TPU v7x, 32 devices: a whole 2x2x4 slice. The times are simulated.
32 devices in a mesh: dp: 4 (over y, x), ctx: 2 (over core), tensor: 4 (over z).
Axes of the slice: x: 2, y: 2, z: 4, core: 2. Of those that a mesh axis runs over, the one named last changes fastest.
Arguments:
- hidden: bfloat16 [4, 1024, 1408], P('dp', 'ctx'), may hold values from -6 to 6
- long_skip_input: bfloat16 [4, 1024, 1408], P('dp', 'ctx'), may hold values from -6 to 6
- condition: bfloat16 [4, 1408], P('dp'), may hold values from -6 to 6
- projected_text_tokens: bfloat16 [4, 333, 1024], P('dp'), may hold values from -6 to 6
- sequence_adapter_index: int32 [4], P('dp'), may hold values from 0 to 7
- skip_projection_weight: bfloat16 [2816, 1408], P('tensor', 'dp'), may hold values from -0.109375 to 0.109375
- shift_modulation_weight: bfloat16 [1408, 1408], P('dp'), may hold values from -0.15625 to 0.15625
- self_query_weight: bfloat16 [1408, 1408], P('dp', 'tensor'), may hold values from -0.15625 to 0.15625
- self_key_weight: bfloat16 [1408, 1408], P('dp', 'tensor'), may hold values from -0.15625 to 0.15625
- self_value_weight: bfloat16 [1408, 1408], P('dp', 'tensor'), may hold values from -0.15625 to 0.15625
- attention_output_weight: bfloat16 [1408, 1408], P('tensor', 'dp'), may hold values from -0.625 to 0.625
- cross_query_weight: bfloat16 [1408, 1408], P('dp', 'tensor'), may hold values from -0.15625 to 0.15625
- cross_key_weight: bfloat16 [1024, 1408], P('dp', 'tensor'), may hold values from -0.1875 to 0.1875
- cross_value_weight: bfloat16 [1024, 1408], P('dp', 'tensor'), may hold values from -0.1875 to 0.1875
- cross_output_weight: bfloat16 [1408, 1408], P('tensor', 'dp'), may hold values from -0.4375 to 0.4375
- feedforward_up_weight: bfloat16 [1408, 6144], P('dp', 'tensor'), may hold values from -0.15625 to 0.15625
- feedforward_down_weight: bfloat16 [6144, 1408], P('tensor', 'dp'), may hold values from -0.078125 to 0.078125
- skip_norm_gain: float32 [2816], replicated, may hold values from 0.1 to 1.9
- norm_gain_rows: float32 [3, 1408], replicated, may hold values from 0.1 to 1.9
- adapter_down_factor: bfloat16 [8, 16, 22272], replicated, may hold values from -0.15625 to 0.15625
- adapter_up_factor: bfloat16 [8, 16, 21632], replicated, may hold values from -0.75 to 0.75
- cotangent: bfloat16 [4, 1024, 1408], P('dp', 'ctx'), may hold values from -6 to 6
Outputs:
- block_out: bfloat16 [4, 1024, 1408], P('dp', 'ctx')
- hidden_grad: float32 [4, 1024, 1408], P('dp', 'ctx')
- skip_grad: float32 [4, 1024, 1408], P('dp', 'ctx')
- condition_gradient: float32 [5632], P(('dp', 'ctx', 'tensor'))
- adapter_down_gradient: float32 [2850816], P(('dp', 'ctx', 'tensor'))
- adapter_up_gradient: float32 [2768896], P(('dp', 'ctx', 'tensor'))
Inputs may be any that keep to these rules, and one draw needn't show every extreme that they name: `sequence_adapter_index`: the adapter of each sequence, one of 8.
All inputs are finite; a program needn't handle non-finite values.
Results may differ from a plain program's by a relative error of at most 0.024.
Values may be sent and summed in bfloat16 or wider, within the bound.
A program may use at most 192 MiB of HBM per device.

v0:
```python
from functools import partial

import jax
import jax.numpy as jnp
from jax import lax
from jax.experimental import pallas as pl
from jax.experimental.pallas import tpu as pltpu
from jax.sharding import PartitionSpec as P

MODEL_WIDTH = 1408
HD = 88
FF = 6144
TW = 1024


PRECISE = lax.Precision.HIGHEST
NORM_EPS = 1e-06


def row_norm(values):
    centered = values - jnp.mean(values, axis=-1, keepdims=True)
    inverse = lax.rsqrt(jnp.mean(centered * centered, axis=-1, keepdims=True) + NORM_EPS)
    return (centered * inverse, inverse)


def head_norm(values, head_width):
    shaped = values.reshape(values.shape[:-1] + (values.shape[-1] // head_width, head_width))
    centered = shaped - jnp.mean(shaped, axis=-1, keepdims=True)
    inverse = lax.rsqrt(jnp.mean(centered * centered, axis=-1, keepdims=True) + NORM_EPS)
    return (centered * inverse, inverse)


def norm_back(normal, inverse, grad_normal):
    return inverse * (
        grad_normal
        - jnp.mean(grad_normal, axis=-1, keepdims=True)
        - normal * jnp.mean(grad_normal * normal, axis=-1, keepdims=True)
    )


def split_parts(values):
    if values.dtype == jnp.bfloat16:
        return [values]
    upper_half = values.astype(jnp.bfloat16)
    lower_half = (values - upper_half.astype(jnp.float32)).astype(jnp.bfloat16)
    return [upper_half, lower_half]


def paired_product(form, left, right):
    total = None
    for left_number, left_part in enumerate(split_parts(left)):
        for right_number, right_part in enumerate(split_parts(right)):
            if left_number + right_number < 2:
                term = jnp.einsum(form, left_part, right_part, preferred_element_type=jnp.float32)
                total = term if total is None else total + term
    return total


def lowrank_out(input_list, weight_matrix, down_piece, up_factor_piece):
    frozen_term = jnp.einsum(
        "gtb,bx->gtx", input_list, weight_matrix, preferred_element_type=jnp.float32
    )
    rank_activation = jnp.einsum(
        "snd,srd->snr", input_list, down_piece, preferred_element_type=jnp.float32
    )
    adapter_term = paired_product("dti,dip->dtp", rank_activation, up_factor_piece)
    return (frozen_term + adapter_term, rank_activation)


def lowrank_back(
    input_list,
    weight_matrix,
    down_piece,
    up_factor_piece,
    rank_activation,
    output_gradient,
    want_input,
):
    upper_gradient = paired_product("pmf,pmz->pfz", rank_activation, output_gradient)
    rank_gradient = paired_product("hzu,hlu->hzl", output_gradient, up_factor_piece)
    grad_lower = paired_product("snr,snd->srd", rank_gradient, input_list)
    if want_input:
        input_gradients = paired_product("lga,wa->lgw", output_gradient, weight_matrix)
        input_gradients = input_gradients + paired_product(
            "snr,srd->snd", rank_gradient, down_piece
        )
        return (input_gradients, grad_lower, upper_gradient)
    return (None, grad_lower, upper_gradient)


def attend_forward(query, key_rows, values_in, scale_factor):
    scores = (
        jnp.einsum("snhe,smhe->shnm", query, key_rows, preferred_element_type=jnp.float32)
        * scale_factor
    )
    row_top = jnp.max(scores, axis=-1, keepdims=True)
    exp_scores = jnp.exp(scores - row_top)
    row_total = jnp.sum(exp_scores, axis=-1, keepdims=True)
    attn_probs = (exp_scores / row_total).astype(jnp.bfloat16)
    result = jnp.einsum(
        "shnm,smhe->snhe", attn_probs, values_in, preferred_element_type=jnp.float32
    )
    return (result, row_top + jnp.log(row_total))


def attend_back(query, key_rows, values_in, log_total, grad_result, scale_factor):
    scores = (
        jnp.einsum("snhe,smhe->shnm", query, key_rows, preferred_element_type=jnp.float32)
        * scale_factor
    )
    attn_probs = jnp.exp(scores - log_total)
    grad_probs = jnp.einsum(
        "snhe,smhe->shnm", grad_result, values_in, preferred_element_type=jnp.float32
    )
    row_inner = jnp.sum(attn_probs * grad_probs, axis=-1, keepdims=True)
    grad_scores = (attn_probs * (grad_probs - row_inner)).astype(jnp.bfloat16)
    grad_query = (
        jnp.einsum("shnm,smhe->snhe", grad_scores, key_rows, preferred_element_type=jnp.float32)
        * scale_factor
    )
    grad_keys = (
        jnp.einsum("shnm,snhe->smhe", grad_scores, query, preferred_element_type=jnp.float32)
        * scale_factor
    )
    grad_values = jnp.einsum(
        "shnm,snhe->smhe",
        attn_probs.astype(jnp.bfloat16),
        grad_result,
        preferred_element_type=jnp.float32,
    )
    return (grad_query, grad_keys, grad_values)


def body(
    hidden,
    long_skip_input,
    condition,
    projected_text_tokens,
    sequence_adapter_index,
    skip_projection_weight,
    shift_modulation_weight,
    self_query_weight,
    self_key_weight,
    self_value_weight,
    attention_output_weight,
    cross_query_weight,
    cross_key_weight,
    cross_value_weight,
    cross_output_weight,
    feedforward_up_weight,
    feedforward_down_weight,
    skip_norm_gain,
    norm_gain_rows,
    adapter_down_factor,
    adapter_up_factor,
    cotangent,
):
    (
        skip_projection_weight,
        shift_modulation_weight,
        self_query_weight,
        self_key_weight,
        self_value_weight,
        attention_output_weight,
        cross_query_weight,
        cross_key_weight,
        cross_value_weight,
        cross_output_weight,
        feedforward_up_weight,
        feedforward_down_weight,
    ) = (
        lax.all_gather(skip_projection_weight, "dp", axis=1, tiled=True),
        lax.all_gather(shift_modulation_weight, "dp", axis=0, tiled=True),
        lax.all_gather(self_query_weight, "dp", axis=0, tiled=True),
        lax.all_gather(self_key_weight, "dp", axis=0, tiled=True),
        lax.all_gather(self_value_weight, "dp", axis=0, tiled=True),
        lax.all_gather(attention_output_weight, "dp", axis=1, tiled=True),
        lax.all_gather(cross_query_weight, "dp", axis=0, tiled=True),
        lax.all_gather(cross_key_weight, "dp", axis=0, tiled=True),
        lax.all_gather(cross_value_weight, "dp", axis=0, tiled=True),
        lax.all_gather(cross_output_weight, "dp", axis=1, tiled=True),
        lax.all_gather(feedforward_up_weight, "dp", axis=0, tiled=True),
        lax.all_gather(feedforward_down_weight, "dp", axis=1, tiled=True),
    )
    tensor_rank = lax.axis_index("tensor")
    tensor_count = lax.axis_size("tensor")
    seqs_local = hidden.shape[0]
    tokens_local = hidden.shape[1]
    local_width = self_query_weight.shape[1]
    heads_local = local_width // HD
    ff_local = feedforward_up_weight.shape[1]
    skip_width = skip_projection_weight.shape[0]
    scale_factor = HD ** (-0.5)
    in_sizes = [
        2 * MODEL_WIDTH,
        MODEL_WIDTH,
        MODEL_WIDTH,
        MODEL_WIDTH,
        MODEL_WIDTH,
        MODEL_WIDTH,
        MODEL_WIDTH,
        TW,
        TW,
        MODEL_WIDTH,
        MODEL_WIDTH,
        FF,
    ]
    out_sizes = [MODEL_WIDTH] * 10 + [FF, MODEL_WIDTH]
    input_offsets = [sum(in_sizes[:number]) for number in range(12)]
    output_offsets = [sum(out_sizes[:number]) for number in range(12)]
    select_adapter = (
        sequence_adapter_index[:, None]
        == jnp.arange(adapter_down_factor.shape[0], dtype=jnp.int32)[None, :]
    )
    choose_wide = select_adapter.astype(jnp.float32)
    down_seq = jnp.einsum(
        "fn,nge->fge",
        select_adapter.astype(jnp.bfloat16),
        adapter_down_factor,
        preferred_element_type=jnp.float32,
    ).astype(jnp.bfloat16)
    up_seq = jnp.einsum(
        "fn,nge->fge",
        select_adapter.astype(jnp.bfloat16),
        adapter_up_factor,
        preferred_element_type=jnp.float32,
    ).astype(jnp.bfloat16)

    def down_full(number):
        return down_seq[:, :, input_offsets[number] : input_offsets[number] + in_sizes[number]]

    def up_full(number):
        return up_seq[:, :, output_offsets[number] : output_offsets[number] + out_sizes[number]]

    def down_local(number, span_width):
        return lax.dynamic_slice_in_dim(
            down_seq, input_offsets[number] + tensor_rank * span_width, span_width, 2
        )

    def up_local(number, span_width):
        return lax.dynamic_slice_in_dim(
            up_seq, output_offsets[number] + tensor_rank * span_width, span_width, 2
        )

    def to_slots(grad_piece):
        return jnp.einsum("si,srd->ird", choose_wide, grad_piece, precision=PRECISE)

    joined = jnp.concatenate([hidden, long_skip_input], axis=-1).astype(jnp.float32)
    joined_normal, joined_inverse = row_norm(joined)
    joined_low = (joined_normal * skip_norm_gain).astype(jnp.bfloat16)
    joined_part = lax.dynamic_slice_in_dim(joined_low, tensor_rank * skip_width, skip_width, 2)
    skip_partial, skip_rank = lowrank_out(
        joined_part, skip_projection_weight, down_local(0, skip_width), up_full(0)
    )
    skip_out = lax.psum(skip_partial.astype(jnp.bfloat16), "tensor").astype(jnp.float32)
    act_wide, silu_pull = jax.vjp(jax.nn.silu, condition.astype(jnp.float32))
    act_low = act_wide.astype(jnp.bfloat16)[:, None, :]
    shift_row, mod_rank = lowrank_out(act_low, shift_modulation_weight, down_full(1), up_full(1))
    first_normal, first_inverse = row_norm(skip_out)
    attn_in = (first_normal * norm_gain_rows[0] + shift_row).astype(jnp.bfloat16)
    query_proj, query_rank = lowrank_out(
        attn_in, self_query_weight, down_full(2), up_local(2, local_width)
    )
    key_proj, key_rank = lowrank_out(
        attn_in, self_key_weight, down_full(3), up_local(3, local_width)
    )
    value_proj, value_rank = lowrank_out(
        attn_in, self_value_weight, down_full(4), up_local(4, local_width)
    )
    query_normal, query_inverse = head_norm(query_proj, HD)
    key_normal, key_inverse = head_norm(key_proj, HD)
    query_low = query_normal.astype(jnp.bfloat16)
    key_low = key_normal.astype(jnp.bfloat16).reshape(seqs_local, tokens_local, local_width)
    value_low = value_proj.astype(jnp.bfloat16)
    keys_all, values_all = (
        lax.all_gather(key_low, "ctx", axis=1, tiled=True),
        lax.all_gather(value_low, "ctx", axis=1, tiled=True),
    )
    keys_four = keys_all.reshape(seqs_local, -1, heads_local, HD)
    values_four = values_all.reshape(seqs_local, -1, heads_local, HD)
    attn_result, attn_log = attend_forward(query_low, keys_four, values_four, scale_factor)
    attn_low = attn_result.reshape(seqs_local, tokens_local, local_width).astype(jnp.bfloat16)
    attn_partial, out_rank = lowrank_out(
        attn_low, attention_output_weight, down_local(5, local_width), up_full(5)
    )
    first_res = skip_out + lax.psum(attn_partial.astype(jnp.bfloat16), "tensor").astype(jnp.float32)
    second_normal, second_inverse = row_norm(first_res)
    cross_in = (second_normal * norm_gain_rows[1]).astype(jnp.bfloat16)
    cquery_proj, cquery_rank = lowrank_out(
        cross_in, cross_query_weight, down_full(6), up_local(6, local_width)
    )
    ckey_proj, ckey_rank = lowrank_out(
        projected_text_tokens, cross_key_weight, down_full(7), up_local(7, local_width)
    )
    cvalue_proj, cvalue_rank = lowrank_out(
        projected_text_tokens, cross_value_weight, down_full(8), up_local(8, local_width)
    )
    cquery_normal, cquery_inverse = head_norm(cquery_proj, HD)
    ckey_normal, ckey_inverse = head_norm(ckey_proj, HD)
    cquery_low = cquery_normal.astype(jnp.bfloat16)
    ckey_low = ckey_normal.astype(jnp.bfloat16)
    cvalue_low = cvalue_proj.astype(jnp.bfloat16).reshape(seqs_local, -1, heads_local, HD)
    cross_result, cross_log = attend_forward(cquery_low, ckey_low, cvalue_low, scale_factor)
    cross_low = cross_result.reshape(seqs_local, tokens_local, local_width).astype(jnp.bfloat16)
    cross_partial, cout_rank = lowrank_out(
        cross_low, cross_output_weight, down_local(9, local_width), up_full(9)
    )
    second_res = first_res + lax.psum(cross_partial.astype(jnp.bfloat16), "tensor").astype(
        jnp.float32
    )
    third_normal, third_inverse = row_norm(second_res)
    mlp_in = (third_normal * norm_gain_rows[2]).astype(jnp.bfloat16)
    up_proj, up_rank = lowrank_out(
        mlp_in, feedforward_up_weight, down_full(10), up_local(10, ff_local)
    )
    activated, gelu_pull = jax.vjp(partial(jax.nn.gelu, approximate=True), up_proj)
    activated_low = activated.astype(jnp.bfloat16)
    down_partial, down_rank = lowrank_out(
        activated_low, feedforward_down_weight, down_local(11, ff_local), up_full(11)
    )
    block_out = second_res + lax.psum(down_partial.astype(jnp.bfloat16), "tensor").astype(
        jnp.float32
    )
    grad_act, grad_down_lower, grad_down_upper = lowrank_back(
        activated_low,
        feedforward_down_weight,
        down_local(11, ff_local),
        up_full(11),
        down_rank,
        cotangent,
        True,
    )
    grad_pre = gelu_pull(grad_act)[0].astype(jnp.bfloat16)
    grad_mlp_in, grad_up_lower, grad_up_upper = lowrank_back(
        mlp_in,
        feedforward_up_weight,
        down_full(10),
        up_local(10, ff_local),
        up_rank,
        grad_pre,
        True,
    )
    grad_mlp_in = lax.psum(grad_mlp_in.astype(jnp.bfloat16), "tensor").astype(jnp.float32)
    grad_second = cotangent.astype(jnp.float32) + norm_back(
        third_normal, third_inverse, grad_mlp_in * norm_gain_rows[2]
    )
    grad_cross_low, grad_cout_lower, grad_cout_upper = lowrank_back(
        cross_low,
        cross_output_weight,
        down_local(9, local_width),
        up_full(9),
        cout_rank,
        grad_second.astype(jnp.bfloat16),
        True,
    )
    grad_cross_result = grad_cross_low.astype(jnp.bfloat16).reshape(
        seqs_local, tokens_local, heads_local, HD
    )
    grad_cquery, grad_ckey, grad_cvalue = attend_back(
        cquery_low, ckey_low, cvalue_low, cross_log, grad_cross_result, scale_factor
    )
    grad_cquery_proj = (
        norm_back(cquery_normal, cquery_inverse, grad_cquery)
        .reshape(seqs_local, tokens_local, local_width)
        .astype(jnp.bfloat16)
    )
    grad_ckey_proj = norm_back(ckey_normal, ckey_inverse, grad_ckey).reshape(
        seqs_local, -1, local_width
    )
    none_first, grad_ckey_lower, grad_ckey_upper = lowrank_back(
        projected_text_tokens,
        cross_key_weight,
        down_full(7),
        up_local(7, local_width),
        ckey_rank,
        grad_ckey_proj,
        False,
    )
    none_second, grad_cvalue_lower, grad_cvalue_upper = lowrank_back(
        projected_text_tokens,
        cross_value_weight,
        down_full(8),
        up_local(8, local_width),
        cvalue_rank,
        grad_cvalue.reshape(seqs_local, -1, local_width),
        False,
    )
    grad_cross_in, grad_cquery_lower, grad_cquery_upper = lowrank_back(
        cross_in,
        cross_query_weight,
        down_full(6),
        up_local(6, local_width),
        cquery_rank,
        grad_cquery_proj,
        True,
    )
    grad_cross_in = lax.psum(grad_cross_in.astype(jnp.bfloat16), "tensor").astype(jnp.float32)
    grad_first = grad_second + norm_back(
        second_normal, second_inverse, grad_cross_in * norm_gain_rows[1]
    )
    grad_attn_low, grad_aout_lower, grad_aout_upper = lowrank_back(
        attn_low,
        attention_output_weight,
        down_local(5, local_width),
        up_full(5),
        out_rank,
        grad_first.astype(jnp.bfloat16),
        True,
    )
    grad_attn_result = grad_attn_low.astype(jnp.bfloat16).reshape(
        seqs_local, tokens_local, heads_local, HD
    )
    grad_query, grad_keys_all, grad_values_all = attend_back(
        query_low, keys_four, values_four, attn_log, grad_attn_result, scale_factor
    )
    grad_keys, grad_values = (
        lax.psum_scatter(
            grad_keys_all.reshape(seqs_local, -1, local_width).astype(jnp.bfloat16),
            "ctx",
            scatter_dimension=1,
            tiled=True,
        ).astype(jnp.float32),
        lax.psum_scatter(
            grad_values_all.reshape(seqs_local, -1, local_width).astype(jnp.bfloat16),
            "ctx",
            scatter_dimension=1,
            tiled=True,
        ).astype(jnp.float32),
    )
    grad_query_proj = (
        norm_back(query_normal, query_inverse, grad_query)
        .reshape(seqs_local, tokens_local, local_width)
        .astype(jnp.bfloat16)
    )
    grad_key_proj = (
        norm_back(
            key_normal, key_inverse, grad_keys.reshape(seqs_local, tokens_local, heads_local, HD)
        )
        .reshape(seqs_local, tokens_local, local_width)
        .astype(jnp.bfloat16)
    )
    grad_value_proj = grad_values.astype(jnp.bfloat16)
    grad_in_query, grad_query_lower, grad_query_upper = lowrank_back(
        attn_in,
        self_query_weight,
        down_full(2),
        up_local(2, local_width),
        query_rank,
        grad_query_proj,
        True,
    )
    grad_in_key, grad_key_lower, grad_key_upper = lowrank_back(
        attn_in,
        self_key_weight,
        down_full(3),
        up_local(3, local_width),
        key_rank,
        grad_key_proj,
        True,
    )
    grad_in_value, grad_value_lower, grad_value_upper = lowrank_back(
        attn_in,
        self_value_weight,
        down_full(4),
        up_local(4, local_width),
        value_rank,
        grad_value_proj,
        True,
    )
    grad_attn_in = lax.psum(
        (grad_in_query + grad_in_key + grad_in_value).astype(jnp.bfloat16), "tensor"
    ).astype(jnp.float32)
    grad_shift = jnp.sum(grad_attn_in, axis=1, keepdims=True) / tensor_count
    grad_act_low, grad_mod_lower, grad_mod_upper = lowrank_back(
        act_low, shift_modulation_weight, down_full(1), up_full(1), mod_rank, grad_shift, True
    )
    grad_condition = silu_pull(grad_act_low[:, 0, :])[0]
    grad_skip_out = grad_first + norm_back(
        first_normal, first_inverse, grad_attn_in * norm_gain_rows[0]
    )
    grad_joined_part, grad_skip_lower, grad_skip_upper = lowrank_back(
        joined_part,
        skip_projection_weight,
        down_local(0, skip_width),
        up_full(0),
        skip_rank,
        grad_skip_out.astype(jnp.bfloat16),
        True,
    )
    grad_joined = lax.all_gather(
        grad_joined_part.astype(jnp.bfloat16), "tensor", axis=2, tiled=True
    ).astype(grad_joined_part.dtype)
    grad_joined_full = norm_back(joined_normal, joined_inverse, grad_joined * skip_norm_gain)
    hidden_grad = grad_joined_full[:, :, :MODEL_WIDTH]
    skip_grad = grad_joined_full[:, :, MODEL_WIDTH:]
    lower_factor_parts = [
        (0, grad_skip_lower, True),
        (1, grad_mod_lower, False),
        (2, grad_query_lower, False),
        (3, grad_key_lower, False),
        (4, grad_value_lower, False),
        (5, grad_aout_lower, True),
        (6, grad_cquery_lower, False),
        (7, grad_ckey_lower, False),
        (8, grad_cvalue_lower, False),
        (9, grad_cout_lower, True),
        (10, grad_up_lower, False),
        (11, grad_down_lower, True),
    ]
    upper_factor_parts = [
        (0, grad_skip_upper, False),
        (1, grad_mod_upper, False),
        (2, grad_query_upper, True),
        (3, grad_key_upper, True),
        (4, grad_value_upper, True),
        (5, grad_aout_upper, False),
        (6, grad_cquery_upper, True),
        (7, grad_ckey_upper, True),
        (8, grad_cvalue_upper, True),
        (9, grad_cout_upper, False),
        (10, grad_up_upper, True),
        (11, grad_down_upper, False),
    ]
    slot_total = adapter_down_factor.shape[0]
    rank_total = adapter_down_factor.shape[1]
    cond_buffer = jnp.zeros((lax.axis_size("dp") * seqs_local, MODEL_WIDTH), jnp.float32)
    cond_buffer = lax.dynamic_update_slice_in_dim(
        cond_buffer, grad_condition, lax.axis_index("dp") * seqs_local, 0
    )
    cond_flat = cond_buffer.reshape(-1)

    def dense_table(parts_list, starts, total_width, row_count, slot_pieces):
        table = jnp.zeros((row_count, total_width), jnp.float32)
        for position, (number, grad_piece, is_local) in enumerate(parts_list):
            span_width = grad_piece.shape[2]
            column_start = starts[number] + tensor_rank * span_width if is_local else starts[number]
            table = lax.dynamic_update_slice_in_dim(table, slot_pieces[position], column_start, 1)
        return table

    down_factor_slots = [
        to_slots(grad_piece).reshape(slot_total * rank_total, -1)
        for number, grad_piece, is_local in lower_factor_parts
    ]
    up_factor_slots = [
        to_slots(grad_piece).reshape(slot_total * rank_total, -1)
        for number, grad_piece, is_local in upper_factor_parts
    ]
    down_compact = jnp.concatenate(down_factor_slots, axis=1)
    up_compact = jnp.concatenate(up_factor_slots, axis=1)
    cond_rows, down_rows, up_rows = (
        lax.psum_scatter(
            cond_flat.astype(jnp.bfloat16), ("dp", "ctx"), scatter_dimension=0, tiled=True
        ).astype(jnp.float32),
        lax.psum_scatter(
            down_compact.astype(jnp.bfloat16), ("dp", "ctx"), scatter_dimension=0, tiled=True
        ).astype(jnp.float32),
        lax.psum_scatter(
            up_compact.astype(jnp.bfloat16), ("dp", "ctx"), scatter_dimension=0, tiled=True
        ).astype(jnp.float32),
    )
    row_count = down_rows.shape[0]
    down_widths = [grad_piece.shape[2] for number, grad_piece, is_local in lower_factor_parts]
    up_widths = [grad_piece.shape[2] for number, grad_piece, is_local in upper_factor_parts]
    down_pieces = [
        down_rows[:, sum(down_widths[:position]) : sum(down_widths[: position + 1])]
        for position in range(12)
    ]
    up_pieces = [
        up_rows[:, sum(up_widths[:position]) : sum(up_widths[: position + 1])]
        for position in range(12)
    ]
    down_block = dense_table(
        lower_factor_parts, input_offsets, adapter_down_factor.shape[2], row_count, down_pieces
    ).reshape(-1)
    up_block = dense_table(
        upper_factor_parts, output_offsets, adapter_up_factor.shape[2], row_count, up_pieces
    ).reshape(-1)
    condition_gradient, adapter_down_gradient, adapter_up_gradient = (
        lax.psum_scatter(
            cond_rows.astype(jnp.bfloat16), "tensor", scatter_dimension=0, tiled=True
        ).astype(jnp.float32),
        lax.psum_scatter(
            down_block.astype(jnp.bfloat16), "tensor", scatter_dimension=0, tiled=True
        ).astype(jnp.float32),
        lax.psum_scatter(
            up_block.astype(jnp.bfloat16), "tensor", scatter_dimension=0, tiled=True
        ).astype(jnp.float32),
    )
    return (
        block_out.astype(jnp.bfloat16),
        hidden_grad,
        skip_grad,
        condition_gradient,
        adapter_down_gradient,
        adapter_up_gradient,
    )


BF = jnp.bfloat16
F32 = jnp.float32
MESH_ID = pl.DeviceIdType.MESH
RANK = 16
CHUNK = 64
VMEM_BYTES = 60 << 20


def dot_nn(left, right):
    return jnp.dot(left, right, preferred_element_type=F32)


def dot_nt(left, right):
    return lax.dot_general(left, right, (((1,), (1,)), ((), ())), preferred_element_type=F32)


def dot_tn(left, right):
    return lax.dot_general(left, right, (((0,), (0,)), ((), ())), preferred_element_type=F32)


def stats(values):
    centered = values - jnp.mean(values, axis=-1, keepdims=True)
    inverse = lax.rsqrt(jnp.mean(centered * centered, axis=-1, keepdims=True) + NORM_EPS)
    return centered * inverse, inverse


def greet_all(partners):
    barrier = pltpu.get_barrier_semaphore()
    for condition, device in partners:
        @pl.when(condition)
        def _(device=device):
            pl.semaphore_signal(barrier, inc=1, device_id=device, device_id_type=MESH_ID)


def await_all(partners):
    expected = sum(jnp.where(condition, 1, 0) for condition, _ in partners)
    pl.semaphore_wait(pltpu.get_barrier_semaphore(), expected)


def greet(partners):
    greet_all(partners)
    await_all(partners)


def line_partners(me, count):
    return [(me > 0, {"tensor": lax.max(me - 1, 0)}), (me < count - 1, {"tensor": lax.min(me + 1, count - 1)})]


def push(source, target, send_sem, recv_sem, device):
    return pltpu.make_async_remote_copy(
        src_ref=source,
        dst_ref=target,
        send_sem=send_sem,
        recv_sem=recv_sem,
        device_id=device,
        device_id_type=MESH_ID,
    )


class Line:
    def __init__(self, me, count, send_right, recv_left, send_left, recv_right):
        self.me, self.count = me, count
        self.sems = (send_right, recv_left, send_left, recv_right)
        self.left = {"tensor": lax.max(me - 1, 0)}
        self.right = {"tensor": lax.min(me + 1, count - 1)}
        self.has_left, self.has_right = me > 0, me < count - 1

    def to_right(self, source, target, slot):
        return push(source, target, self.sems[0].at[slot], self.sems[1].at[slot], self.right)

    def to_left(self, source, target, slot):
        return push(source, target, self.sems[2].at[slot], self.sems[3].at[slot], self.left)


def line_reduce_all(line, steps, compute, partial_ref, from_left, from_right, stage_right, stage_left, finish,
                    beside=None, after=None):
    me, count = line.me, line.count
    far = count - 1 - me

    def step(number, carry):
        @pl.when(number < steps)
        def _():
            compute(number)

        slot_r = number - me

        @pl.when((slot_r >= 0) & (slot_r < steps))
        def _():
            slot = lax.clamp(0, slot_r, steps - 1)

            @pl.when(line.has_left)
            def _():
                line.to_right(stage_right.at[slot], from_left.at[slot], slot).wait_recv()

            @pl.when(line.has_right)
            def _():
                @pl.when(line.has_left)
                def _():
                    total = partial_ref[slot].astype(F32) + from_left[slot].astype(F32)
                    stage_right[slot] = total.astype(BF)

                @pl.when(jnp.logical_not(line.has_left))
                def _():
                    stage_right[slot] = partial_ref[slot]

                line.to_right(stage_right.at[slot], from_left.at[slot], slot).start()

        slot_l = number - far

        @pl.when((slot_l >= 0) & (slot_l < steps))
        def _():
            slot = lax.clamp(0, slot_l, steps - 1)

            @pl.when(line.has_right)
            def _():
                line.to_left(stage_left.at[slot], from_right.at[slot], slot).wait_recv()

            @pl.when(line.has_left)
            def _():
                @pl.when(line.has_right)
                def _():
                    total = partial_ref[slot].astype(F32) + from_right[slot].astype(F32)
                    stage_left[slot] = total.astype(BF)

                @pl.when(jnp.logical_not(line.has_right))
                def _():
                    stage_left[slot] = partial_ref[slot]

                line.to_left(stage_left.at[slot], from_right.at[slot], slot).start()

        if beside is not None:
            beside(number)
        slot_f = number - lax.max(me, far)

        @pl.when((slot_f >= 0) & (slot_f < steps))
        def _():
            slot = lax.clamp(0, slot_f, steps - 1)

            @pl.when(jnp.logical_not(line.has_left))
            def _():
                finish(slot, partial_ref[slot].astype(F32) + from_right[slot].astype(F32))

            @pl.when(line.has_left)
            def _():
                @pl.when(line.has_right)
                def _():
                    finish(
                        slot,
                        partial_ref[slot].astype(F32)
                        + from_left[slot].astype(F32)
                        + from_right[slot].astype(F32),
                    )

                @pl.when(jnp.logical_not(line.has_right))
                def _():
                    finish(slot, partial_ref[slot].astype(F32) + from_left[slot].astype(F32))

            if after is not None:
                after(slot)

        return carry

    lax.fori_loop(0, steps + count - 1, step, 0)

    def drain(slot, carry):
        @pl.when(line.has_right)
        def _():
            line.to_right(stage_right.at[slot], from_left.at[slot], slot).wait_send()

        @pl.when(line.has_left)
        def _():
            line.to_left(stage_left.at[slot], from_right.at[slot], slot).wait_send()

        return carry

    lax.fori_loop(0, steps, drain, 0)


def scatter_order(me, count, place):
    near = lax.min(me, count - 1 - me)
    base = count - 1 - 2 * near
    index = place - base
    block = jnp.where(
        place < base,
        count - 1 - place,
        jnp.where(index % 2 == 0, 2 * near - index // 2, index // 2),
    )
    return jnp.where(2 * me > count - 1, count - 1 - block, block)


def line_scatter_step(line, number, partial_ref, from_left, from_right, stage_right, stage_left):
    me, count = line.me, line.count
    block_r = count - 1 - number + me

    @pl.when((number >= me) & line.has_right & (block_r > me))
    def _():
        block = lax.clamp(0, block_r, count - 1)

        @pl.when(line.has_left)
        def _():
            line.to_right(stage_right.at[block], from_left.at[block], block).wait_recv()
            total = partial_ref[block].astype(F32) + from_left[block].astype(F32)
            stage_right[block] = total.astype(BF)

        @pl.when(jnp.logical_not(line.has_left))
        def _():
            stage_right[block] = partial_ref[block]

        line.to_right(stage_right.at[block], from_left.at[block], block).start()

    block_l = number - (count - 1 - me)

    @pl.when((block_l >= 0) & line.has_left & (block_l < me))
    def _():
        block = lax.clamp(0, block_l, count - 1)

        @pl.when(line.has_right)
        def _():
            line.to_left(stage_left.at[block], from_right.at[block], block).wait_recv()
            total = partial_ref[block].astype(F32) + from_right[block].astype(F32)
            stage_left[block] = total.astype(BF)

        @pl.when(jnp.logical_not(line.has_right))
        def _():
            stage_left[block] = partial_ref[block]

        line.to_left(stage_left.at[block], from_right.at[block], block).start()


def line_scatter_finish(line, partial_ref, from_left, from_right, stage_right, stage_left, total_ref):
    me, count = line.me, line.count
    total_ref[...] = partial_ref[me].astype(F32)

    @pl.when(line.has_left)
    def _():
        line.to_right(stage_right.at[me], from_left.at[me], me).wait_recv()
        total_ref[...] += from_left[me].astype(F32)

    @pl.when(line.has_right)
    def _():
        line.to_left(stage_left.at[me], from_right.at[me], me).wait_recv()
        total_ref[...] += from_right[me].astype(F32)

    def drain(block, carry):
        @pl.when(block > me)
        def _():
            line.to_right(stage_right.at[block], from_left.at[block], block).wait_send()

        @pl.when(block < me)
        def _():
            line.to_left(stage_left.at[block], from_right.at[block], block).wait_send()

        return carry

    lax.fori_loop(0, count, drain, 0)


def line_gather_step(line, number, slots):
    me, count = line.me, line.count
    block_l = lax.clamp(0, me - number, count - 1)
    block_r = lax.clamp(0, me + number, count - 1)
    view = slots if callable(slots) else lambda block: slots.at[block]

    @pl.when(number <= me)
    def _():
        @pl.when(number > 0)
        def _():
            line.to_right(view(block_l), view(block_l), block_l).wait_recv()

        @pl.when(line.has_right)
        def _():
            line.to_right(view(block_l), view(block_l), block_l).start()

    @pl.when(me + number <= count - 1)
    def _():
        @pl.when(number > 0)
        def _():
            line.to_left(view(block_r), view(block_r), block_r).wait_recv()

        @pl.when(line.has_left)
        def _():
            line.to_left(view(block_r), view(block_r), block_r).start()


def line_gather_drain(line, slots):
    me, count = line.me, line.count
    view = slots if callable(slots) else lambda block: slots.at[block]

    def drain(block, carry):
        @pl.when((block <= me) & line.has_right)
        def _():
            line.to_right(view(block), view(block), block).wait_send()

        @pl.when((block >= me) & line.has_left)
        def _():
            line.to_left(view(block), view(block), block).wait_send()

        return carry

    lax.fori_loop(0, count, drain, 0)


def xor_place(place, number):
    if number == 0:
        return place
    if number == 1:
        return place + 1 - 2 * (place % 2)
    if number == 2:
        return place + 2 - 4 * (place // 2)
    return 3 - place


def call(kernel, inputs, outs, scratch, collective=None, cost=None):
    space = {True: pltpu.VMEM, False: pl.ANY, None: pltpu.SMEM}
    return pl.pallas_call(
        kernel,
        out_shape=[jax.ShapeDtypeStruct(shape, dtype) for shape, dtype, _ in outs],
        in_specs=[pl.BlockSpec(memory_space=space[where]) for _, where in inputs],
        out_specs=[pl.BlockSpec(memory_space=space[where]) for _, _, where in outs],
        scratch_shapes=scratch,
        cost_estimate=cost,
        compiler_params=pltpu.CompilerParams(
            collective_id=collective,
            has_side_effects=collective is not None,
            vmem_limit_bytes=VMEM_BYTES,
        ),
    )(*[array for array, _ in inputs])


def cost_of(flops, moved):
    return pl.CostEstimate(flops=int(flops), bytes_accessed=int(moved), transcendentals=0)


def vmem(*shape, dtype=BF):
    return pltpu.VMEM(shape, dtype)


def dma(*shape):
    return pltpu.SemaphoreType.DMA(shape)


def whole_wait(target, sem):
    pltpu.make_async_copy(target, target, sem).wait()


def rows_of(index, size):
    return pl.ds(pl.multiple_of(index * size, size), size)


IN_SIZES = [2 * MODEL_WIDTH] + [MODEL_WIDTH] * 6 + [TW, TW, MODEL_WIDTH, MODEL_WIDTH, FF]
OUT_SIZES = [MODEL_WIDTH] * 10 + [FF, MODEL_WIDTH]
IN_AT = [sum(IN_SIZES[:number]) for number in range(13)]
OUT_AT = [sum(OUT_SIZES[:number]) for number in range(13)]


def down_of(table, number):
    return table[:, IN_AT[number] : IN_AT[number + 1]]


def up_of(table, number):
    return table[:, OUT_AT[number] : OUT_AT[number + 1]]


def take_local(target, table, start, me, count):
    size = target.shape[-1]
    for place in range(count):
        @pl.when(me == place)
        def _(place=place):
            target[...] = table[:, start + place * size : start + (place + 1) * size]


def take_stack(target, table, start, count):
    size = target.shape[-1]
    for place in range(count):
        target[place] = table[:, start + place * size : start + (place + 1) * size]


def norm_backward(normal, inverse, grad):
    return inverse * (
        grad
        - jnp.mean(grad, axis=-1, keepdims=True)
        - normal * jnp.mean(grad * normal, axis=-1, keepdims=True)
    )


def middle(count, heads, summed, skip_out, query_weight, out_weight, up_weight, down_piece, skip_piece, text_kv, text,
           cotangent, gains, tables):
    share, width = summed.shape
    tokens = skip_out.shape[0]
    local = query_weight.shape[-1]
    units = up_weight.shape[1]
    words, text_width = text.shape
    rows, span = skip_piece.shape
    scale = HD ** (-0.5)
    part_rows = share // 2
    wide = count * part_rows

    def kernel(sum_ref, skip_hbm, q_hbm, o_hbm, u_hbm, d_own, piece, kv_hbm, text_hbm, cot_hbm, gain, dtab, utab,
               g_first, block_sum, ga_q, gb_q, ga_k, gb_k, ga_v, gb_v, ga_o, gb_o, g_ua, g_ub, g_da, g_db, skip_all,
               kv, wq, wo, wu, wd, cot, t_ref, first_ref, second_ref, x_ref, x_low, q_ref, inv_ref, log_ref, low_ref, acc, b_ref, ao,
               bk, bv, ub, da, slots, skip_half, active, grads, u_all, ud_all, gu_all, gd_all, partial_g, left_g, right_g,
               sr_g, sl_g, partial_b, left_b, right_b, sr_b, sl_b, lsem, wsend, wrecv, zsend, zrecv, *sems):
        me = lax.axis_index("tensor")
        core = lax.axis_index("ctx")
        dp = lax.axis_index("dp")
        always = core >= 0
        half = pl.ds(pl.multiple_of(core * (rows // 2), 16), rows // 2)
        down_rows = d_own.shape[0]
        down_half = pl.ds(pl.multiple_of(core * (down_rows // 2), 16), down_rows // 2)
        mine = pl.ds(pl.multiple_of(dp * down_rows, 16), down_rows)
        loads = [
            pltpu.make_async_copy(source, target, lsem.at[number])
            for number, (source, target) in enumerate(
                ((skip_hbm.at[rows_of(me, share), :], first_ref), (piece.at[half, :], skip_half.at[me]), (q_hbm, wq),
                 (o_hbm, wo), (d_own, wd.at[mine, :]), (cot_hbm.at[:, 0], cot.at[0]), (u_hbm.at[mine, :], wu.at[mine, :]), (text_hbm, t_ref),
                 (cot_hbm.at[:, 1], cot.at[1]))
            )
        ]
        z_peers = [{"tensor": xor_place(me, number)} for number in range(1, count)]
        others = [{"dp": xor_place(dp, 1)}, {"dp": xor_place(dp, 2)}, {"ctx": 1 - core}]
        everyone = [(always, device) for device in z_peers + others]
        greet_all(everyone)
        load_kv = pltpu.make_async_copy(kv_hbm, kv, lsem.at[12])
        for load in loads[:4]:
            load.start()
        load_kv.start()
        for load in loads[4:]:
            load.start()
        gather_lines = [Line(me, count, *sems[:4]), Line(me, count, *sems[4:8])]
        grad_lines = [Line(me, count, *sems[8:12]), Line(me, count, *sems[12:16])]
        block_line = Line(me, count, *sems[16:])

        def gather(which, number):
            line_gather_step(gather_lines[which], number, slots.at[which])

        def scatter(which, number):
            line_scatter_step(
                grad_lines[which], number, partial_g.at[which], left_g.at[which], right_g.at[which], sr_g.at[which],
                sl_g.at[which],
            )

        down = Shared(wd, down_rows, (wsend, wrecv, 0))
        up_w = Shared(wu, down_rows, (wsend, wrecv, 2))
        arrived_up = [
            pltpu.make_async_copy(Shared(u_hbm, down_rows, (wsend, wrecv, 2)).view(block, core), up_w.view(block, core),
                                  lsem.at[10 + number])
            for number, block in enumerate((up_w.first, up_w.second))
        ]
        for load in arrived_up:
            load.start()
        skip = Shared(skip_all, rows, (wsend, wrecv, 1), stacked=True)
        await_all(everyone)
        down.send_own(d_own.at[down_half, :])
        z_sends = [
            push(piece.at[half, :], skip_half.at[me], zsend.at[number], zrecv.at[number], device)
            for number, device in enumerate(z_peers)
        ]
        for send in z_sends:
            send.start()
        take_stack(b_ref, utab, OUT_AT[6], count)
        take_stack(ao, dtab, IN_AT[9], count)
        take_stack(bk, utab, OUT_AT[7], count)
        take_stack(bv, utab, OUT_AT[8], count)
        take_local(ub, utab, OUT_AT[10], me, count)
        take_local(da, dtab, IN_AT[11], me, count)

        for load in arrived_up:
            load.wait()
        up_w.forward()
        up_w.swap(0)
        up_w.swap(1)

        loads[0].wait()
        first = first_ref[...] + sum_ref[...]
        first_ref[...] = first
        second_ref[...] = first
        normal, _ = stats(first)
        x = (normal * gain[1:2, :]).astype(BF)
        x_ref[...] = x
        u = dot_nt(x, down_of(dtab, 6)).astype(BF)
        loads[2].wait()
        loads[3].wait()
        load_kv.wait()

        def cross(place, u_low):
            y = dot_nn(x_ref[...], wq[place]) + dot_nn(u, b_ref[place])
            outs, inverses, logs = [], [], []
            for head in range(heads):
                at = slice(head * HD, (head + 1) * HD)
                normal, inverse = stats(y[:, at])
                q = normal.astype(BF)
                q_ref[place, head] = q
                inverses.append(inverse)
                s = dot_nt(q, kv[0, place, :, at]) * scale
                top = jnp.max(s, axis=-1, keepdims=True)
                e = jnp.exp(s - top)
                total = jnp.sum(e, axis=-1, keepdims=True)
                p = (e * (1.0 / total)).astype(BF)
                outs.append(dot_nn(p, kv[1, place, :, at]))
                logs.append(top + jnp.log(total))
            inv_ref[place] = jnp.concatenate(inverses, axis=1)
            log_ref[place] = jnp.concatenate(logs, axis=1)
            low = jnp.concatenate(outs, axis=1).astype(BF)
            low_ref[place] = low
            second_ref[...] += dot_nt(low, wo[place])
            return u_low + dot_nt(low, ao[place])

        u_low = lax.fori_loop(0, count, cross, jnp.zeros((share, RANK), F32)).astype(BF)
        second = second_ref[...] + dot_nn(u_low, up_of(utab, 9))
        second_ref[...] = second
        normal, _ = stats(second)
        x_mlp = (normal * gain[2:3, :]).astype(BF)
        slots[0, me] = x_mlp[:part_rows]
        slots[1, me] = x_mlp[part_rows:]

        gather(0, 0)
        up_w.wait(2)
        up_w.swap(2)
        down.wait(0)
        down.forward()
        down.swap(0)
        down.wait(1)
        down.swap(1)
        gather(0, 1)
        gather(1, 0)
        loads[1].wait()
        for number in range(count - 1):
            arrived = skip_half.at[xor_place(me, number + 1)]
            push(arrived, arrived, zsend.at[number], zrecv.at[number], z_peers[number]).wait_recv()
        skip_place = pltpu.make_async_copy(skip_half, skip.view(dp, core), lsem.at[9])
        skip_place.start()
        skip.send_own(skip_half)
        down.wait(2)
        down.swap(2)
        for number in (4, 5, 6, 8):
            loads[number].wait()
        ua, db = down_of(dtab, 10), up_of(utab, 11)
        gather(0, 2)
        gather(1, 1)
        down.wait_swaps()
        up_w.wait_swaps()

        def part(number):
            return pl.ds(pl.multiple_of(number * wide, wide), wide)

        def first_grads(number, carry):
            ct = cot[number].reshape(wide, width)
            gd = dot_nt(ct, db).astype(BF)
            gd_all[part(number), :] = gd
            grads[part(number), :] = (dot_nn(ct, wd[...]) + dot_nn(gd, da[...])).astype(BF)
            return carry

        lax.fori_loop(0, 1, first_grads, 0)
        gather(0, 3)

        def forward_part(number, carry):
            here = part(number)

            @pl.when(number == 1)
            def _():
                first_grads(1, 0)
                gather(1, 3)
                scatter(0, 1)

            x = slots[number].reshape(wide, width)
            u = dot_nt(x, ua).astype(BF)
            u_all[here, :] = u
            up = dot_nn(x, wu[...]) + dot_nn(u, ub[...])
            square = up * up
            curve = jnp.tanh(0.7978845608028654 * (up + 0.044715 * square * up))
            flat = 0.5 * (1.0 + curve)
            active[here, :] = (up * flat).astype(BF)
            slope = flat + 0.5 * up * (1.0 - curve * curve) * (0.7978845608028654 * (1.0 + 0.134145 * square))
            g_up = (grads[here, :].astype(F32) * slope).astype(BF)
            grads[here, :] = g_up
            gu = dot_nt(g_up, ub[...]).astype(BF)
            gu_all[here, :] = gu
            g_x = (dot_nt(g_up, wu[...]) + dot_nn(gu, ua)).astype(BF)
            partial_g[number] = g_x.reshape(count, part_rows, width)

            @pl.when(number == 0)
            def _():
                scatter(0, 0)
                gather(1, 2)

            return carry

        lax.fori_loop(0, 2, forward_part, 0)
        scatter(0, 2)
        scatter(1, 0)
        skip.wait(0)
        skip.forward()
        skip.wait(1)

        def down_product(number, carry):
            here = part(number)
            act = active[here, :]
            ud = dot_nt(act, da[...]).astype(BF)
            ud_all[here, :] = ud
            y = dot_nt(act, wd[...]) + dot_nn(ud, db)
            piece_rows = rows_of(number, part_rows)
            for block in range(count):
                own = jnp.where(block == me, 1.0, 0.0)
                one = y[block * part_rows : (block + 1) * part_rows] + second_ref[piece_rows, :] * own
                partial_b[block, piece_rows, :] = one.astype(BF)

            @pl.when(number == 0)
            def _():
                scatter(1, 1)

            return carry

        lax.fori_loop(0, 2, down_product, 0)
        scatter(1, 2)
        skip_place.wait()
        skip.swap(0)
        skip.swap(1)
        skip.swap(3)
        line_scatter_step(block_line, 0, partial_b, left_b, right_b, sr_b, sl_b)
        g_ub[...] = dot_tn(u_all[...], grads[...])
        g_ua[...] = dot_tn(gu_all[...], slots[...].reshape(tokens, width))
        g_db[...] = dot_tn(ud_all[...], cot[...].reshape(tokens, width))
        g_da[...] = dot_tn(gd_all[...], active[...])
        loads[7].wait()
        uq = dot_nt(x_ref[...], down_of(dtab, 6)).astype(BF)
        words_in = t_ref[...]
        uk = dot_nt(words_in, down_of(dtab, 7)).astype(BF)
        uv = dot_nt(words_in, down_of(dtab, 8)).astype(BF)
        for which in range(2):
            line_gather_drain(gather_lines[which], slots.at[which])
            line_scatter_finish(
                grad_lines[which], partial_g.at[which], left_g.at[which], right_g.at[which], sr_g.at[which],
                sl_g.at[which], acc.at[which * part_rows : (which + 1) * part_rows, :],
            )
        skip.wait(2)
        skip.swap(2)

        normal, inverse = stats(second_ref[...])
        own_cot = jnp.concatenate([cot[0, me], cot[1, me]], axis=0).astype(F32)
        g_second = own_cot + norm_backward(normal, inverse, acc[...] * gain[2:3, :])
        second_ref[...] = g_second
        g_low = g_second.astype(BF)
        x_low[...] = g_low
        go = dot_nt(g_low, up_of(utab, 9)).astype(BF)
        gb_o[...] = dot_tn(u_low, g_low)
        acc[...] = jnp.zeros_like(acc)

        def cross_grads(place, carry):
            gq_sum, gk_sum, gv_sum = carry

            @pl.when((place > 0) & (place < count - 1))
            def _():
                line_scatter_step(block_line, place, partial_b, left_b, right_b, sr_b, sl_b)

            g_attn = (dot_nn(x_low[...], wo[place]) + dot_nn(go, ao[place])).astype(BF)
            ga_o[place] = dot_tn(go, low_ref[place])
            gq_parts, gk_parts, gv_parts = [], [], []
            for head in range(heads):
                at = slice(head * HD, (head + 1) * HD)
                gh = g_attn[:, at]
                q = q_ref[place, head]
                k = kv[0, place, :, at]
                v = kv[1, place, :, at]
                p = jnp.exp(dot_nt(q, k) * scale - log_ref[place, :, head : head + 1])
                dp_ = dot_nt(gh, v)
                inner = jnp.sum(p * dp_, axis=-1, keepdims=True)
                ds = (p * (dp_ - inner)).astype(BF)
                dq = dot_nn(ds, k) * scale
                dk = dot_tn(ds, q) * scale
                gq_parts.append(norm_backward(q.astype(F32), inv_ref[place, :, head : head + 1], dq))
                side = kv[0, place, :, local + 2 * head : local + 2 * head + 2].astype(F32)
                gk_parts.append(norm_backward(k.astype(F32), side[:, 0:1] + side[:, 1:2], dk))
                gv_parts.append(dot_tn(p.astype(BF), gh))
            gq = jnp.concatenate(gq_parts, axis=1).astype(BF)
            gk = jnp.concatenate(gk_parts, axis=1).astype(BF)
            gv = jnp.concatenate(gv_parts, axis=1).astype(BF)
            acc[...] += dot_nt(gq, wq[place])
            gb_q[place] = dot_tn(uq, gq)
            gb_k[place] = dot_tn(uk, gk)
            gb_v[place] = dot_tn(uv, gv)
            return (
                gq_sum + dot_nt(gq, b_ref[place]),
                gk_sum + dot_nt(gk, bk[place]),
                gv_sum + dot_nt(gv, bv[place]),
            )

        start = (jnp.zeros((share, RANK), F32), jnp.zeros((words, RANK), F32), jnp.zeros((words, RANK), F32))
        gq_sum, gk_sum, gv_sum = lax.fori_loop(0, count, cross_grads, start)
        gq_sum = gq_sum.astype(BF)
        ga_q[...] = dot_tn(gq_sum, x_ref[...])
        ga_k[...] = dot_tn(gk_sum.astype(BF), words_in)
        ga_v[...] = dot_tn(gv_sum.astype(BF), words_in)
        g_x = acc[...] + dot_nn(gq_sum, down_of(dtab, 6))
        normal, inverse = stats(first_ref[...])
        g_first[...] = (second_ref[...] + norm_backward(normal, inverse, g_x * gain[1:2, :])).astype(BF)
        line_scatter_finish(block_line, partial_b, left_b, right_b, sr_b, sl_b, acc)
        block_sum[...] = acc[...].astype(BF)
        skip.wait_swaps()
        skip.drain()
        down.drain()
        up_w.drain_rest()
        for send in z_sends:
            send.wait_send()

    buffers = [vmem(count, share, width) for _ in range(5)]
    return call(
        kernel,
        [(summed, True)]
        + [(array, False) for array in (skip_out, query_weight, out_weight, up_weight, down_piece, skip_piece)]
        + [(text_kv, False), (text, False), (cotangent, False)]
        + [(array, True) for array in (gains, *tables)],
        [
            ((share, width), BF, True),
            ((share, width), BF, True),
            ((RANK, width), F32, True),
            ((count, RANK, local), F32, True),
            ((RANK, text_width), F32, True),
            ((count, RANK, local), F32, True),
            ((RANK, text_width), F32, True),
            ((count, RANK, local), F32, True),
            ((count, RANK, local), F32, True),
            ((RANK, width), F32, True),
            ((RANK, width), F32, True),
            ((RANK, units), F32, True),
            ((RANK, units), F32, True),
            ((RANK, width), F32, True),
            ((count, 4 * rows, span), BF, False),
        ],
        [pltpu.VMEM(text_kv.shape, BF), vmem(count, width, local), vmem(count, width, local), vmem(width, units),
         vmem(width, units), vmem(2, count, part_rows, width), vmem(words, text_width), vmem(share, width, dtype=F32),
         vmem(share, width, dtype=F32), vmem(share, width), vmem(share, width), vmem(count, heads, share, HD), vmem(count, share, heads, dtype=F32),
         vmem(count, share, heads, dtype=F32), vmem(count, share, local), vmem(share, width, dtype=F32)]
        + [vmem(count, RANK, local) for _ in range(4)] + [vmem(RANK, units) for _ in range(2)]
        + [vmem(2, count, part_rows, width), vmem(count, rows // 2, span), vmem(tokens, units), vmem(tokens, units)]
        + [vmem(tokens, RANK) for _ in range(4)] + [vmem(2, count, part_rows, width) for _ in range(5)] + buffers
        + [dma(13), dma(3, 7), dma(3, 7), dma(count), dma(count)] + [dma(count) for _ in range(20)],
        collective=3,
        cost=cost_of(12 * tokens * width * units, 60e6),
    )


class Shared:
    def __init__(self, target, rows, sems, stacked=False, split=True, columns=False):
        self.target, self.rows, self.stacked, self.split, self.columns = target, rows, stacked, split, columns
        self.send_sem, self.recv_sem, self.index = sems
        dp, core = lax.axis_index("dp"), lax.axis_index("ctx")
        self.dp, self.core = dp, core
        self.first = jnp.where(core == 0, xor_place(dp, 1), xor_place(dp, 2))
        self.second = jnp.where(core == 0, xor_place(dp, 2), xor_place(dp, 1))
        self.third = xor_place(dp, 3)

    def view(self, block, which):
        if self.columns:
            return self.target.at[:, pl.ds(pl.multiple_of(block * self.rows, 128), self.rows)]
        size = self.rows // 2 if self.split else self.rows
        start = block * self.rows + (which * size if self.split else 0)
        rows = pl.ds(pl.multiple_of(start, 16), size)
        return self.target.at[:, rows, :] if self.stacked else self.target.at[rows, :]

    def copy(self, number, source, block, which, device):
        target = self.view(block, which)
        source = target if source is None else source
        return push(source, target, self.send_sem.at[self.index, number], self.recv_sem.at[self.index, number], device)

    def send_own(self, source=None):
        self.copy(0, source, self.dp, self.core, {"dp": self.first}).start()
        self.copy(1, source, self.dp, self.core, {"dp": self.second}).start()

    def blocks(self):
        return [self.first, self.second, self.third] + ([self.dp] if self.stacked else [])

    def wait(self, number):
        self.copy(number, None, self.blocks()[number], self.core, {"dp": self.first}).wait_recv()

    def forward(self):
        self.copy(2, None, self.first, self.core, {"dp": self.second}).start()

    def swap(self, number):
        self.copy(3 + number, None, self.blocks()[number], self.core, {"ctx": 1 - self.core}).start()

    def wait_swaps(self):
        other = [self.second, self.first, self.third, self.dp]
        for number in range(len(self.blocks())):
            self.copy(3 + number, None, other[number], 1 - self.core, {"ctx": 1 - self.core}).wait_recv()

    def drain_own(self):
        for number in range(2):
            self.copy(number, None, self.dp, self.core, {"dp": self.first}).wait_send()

    def drain_rest(self):
        for number in range(2, 6):
            self.copy(number, None, self.dp, self.core, {"dp": self.first}).wait_send()

    def drain(self):
        for number in range(3 + (len(self.blocks()) if self.split else 0)):
            self.copy(number, None, self.dp, self.core, {"dp": self.first}).wait_send()


def front(count, heads, condition, index, hidden, long_skip, text, weights, mod_weight, gain_halves, gain_rows, tables):
    tokens, width = hidden.shape
    span = weights["skip"].shape[1]
    words, text_width = text.shape
    local = weights["q"].shape[1]
    units = weights["up"].shape[1]
    share = tokens // count
    block = min(128, tokens)
    chunk = min(CHUNK, tokens)
    pace = max(1, 64 // chunk)
    steps = tokens // chunk
    each = block // chunk
    scale = HD ** (-0.5)
    rows = weights["q"].shape[0]
    text_rows = weights["ck"].shape[1]
    mod_rows = mod_weight.shape[0]

    def kernel(skip_own, q_own, k_own, v_own, o_own, ck_own, cv_own, cq_own, co_own, up_own,
               index_ref, cond, hid_hbm, lsk_hbm, t_hbm, wm_hbm, halves, gain, dtab, utab,
               skip_hbm, attn_hbm, q_out, keys, values, low_out, log_out, inv_q, inv_k, summed, act_all, text_kv,
               wq_hbm, wk_hbm, wv_hbm, wo_hbm, wcq, wco, wup,
               hid, lsk, t_ref, wm, load_sem, skip_out, attn_in, wq, wk, wv, wo, out_sem, shift_row, wskip, wtext, part_x, pgain, sa, tk, tv, qa, qb, kb, vb, oa, mod_in, mod_slice, mod_out, partial_a, left_a, right_a, sr_a, sl_a,
               partial_b, left_b, right_b, sr_b, sl_b, wsend, wrecv, local_sem, msend, mrecv, tsend, trecv,
               xsend, xrecv, *sems):
        me = lax.axis_index("tensor")
        core = lax.axis_index("ctx")
        dp = lax.axis_index("dp")
        always = core >= 0
        peer = {"ctx": 1 - core}
        dp_peers = [{"dp": xor_place(dp, number)} for number in (1, 2, 3)]
        z_peers = [{"tensor": xor_place(me, number)} for number in range(1, count)]
        reduce_line = Line(me, count, *sems[:4])
        scatter_line = Line(me, count, *sems[4:8])
        text_line = Line(me, count, *sems[8:12])
        cross_lines = [Line(me, count, *sems[12:16]), Line(me, count, *sems[16:])]

        def sems_of(number):
            return (wsend, wrecv, number)

        skip = Shared(wskip, rows, sems_of(0))
        shared = {
            name: Shared(target, rows, sems_of(number))
            for name, target, number in (("q", wq, 1), ("k", wk, 2), ("v", wv, 3), ("o", wo, 4))
        }
        words_w = Shared(wtext, text_rows, sems_of(5), split=False, columns=True)
        cross = [Shared(wcq, rows, sems_of(6), stacked=True), Shared(wco, rows, sems_of(7), stacked=True)]
        wide = [Shared(wup, rows, sems_of(8))]
        owns = {"q": q_own, "k": k_own, "v": v_own, "o": o_own}
        half = pl.ds(pl.multiple_of(core * (rows // 2), 16), rows // 2)
        mine = pl.ds(pl.multiple_of(dp * rows, 16), rows)
        my_half = pl.ds(pl.multiple_of(dp * rows + core * (rows // 2), 16), rows // 2)

        everyone = [(always, device) for device in dp_peers + z_peers + [peer]]
        greet_all(everyone)
        loads = [
            pltpu.make_async_copy(source, target, load_sem.at[number])
            for number, (source, target) in enumerate(((hid_hbm, hid), (lsk_hbm, lsk), (t_hbm, t_ref), (wm_hbm, wm)))
        ]

        for place in range(count):
            @pl.when(me == place)
            def _(place=place):
                side = place * span // width
                start = place * span % width
                pgain[...] = halves[side : side + 1, start : start + span]

        places = [
            pltpu.make_async_copy(source, target.at[mine, :], local_sem.at[number])
            for number, (source, target) in enumerate(
                ((skip_own, wskip), (q_own, wq), (k_own, wk), (v_own, wv), (o_own, wo), (up_own, wup))
            )
        ]
        for place in places:
            place.start()
        crossing = [
            pltpu.make_async_copy(source.at[half, :], target.at[me, my_half, :], local_sem.at[7 + number])
            for number, (source, target) in enumerate(((cq_own, wcq), (co_own, wco)))
        ]
        text_mine = pl.ds(pl.multiple_of(dp * text_rows, 128), text_rows)

        def text_place(source):
            return pltpu.make_async_copy(source, wtext.at[:, text_mine], local_sem.at[9])

        @pl.when(core == 0)
        def _():
            text_place(ck_own).start()

        @pl.when(core == 1)
        def _():
            text_place(cv_own).start()

        for place in crossing:
            place.start()
        value = cond[...].astype(F32)
        act_low = (value / (1.0 + jnp.exp(-value))).astype(BF)
        tag = jnp.full((1, 128), index_ref[0], jnp.int32).astype(F32)
        act_all[dp] = jnp.concatenate([act_low.astype(F32), tag], axis=1)
        for load in loads:
            load.start()
        await_all(everyone)
        skip.send_own(skip_own.at[half, :])

        def cross_view(which):
            target = (wcq, wco)[which]
            return lambda block: target.at[block, my_half, :]

        def cross_step(number):
            for which, cross_line in enumerate(cross_lines):
                line_gather_step(cross_line, number, cross_view(which))

        for place in crossing:
            place.wait()
        cross_step(0)
        spread = [
            push(act_all.at[dp], act_all.at[dp], msend.at[0, number], mrecv.at[0, number], device)
            for number, device in enumerate(dp_peers)
        ]
        for copy in spread:
            copy.start()
        take_local(sa, dtab, 0, me, count)
        take_local(tk, utab, OUT_AT[7], me, count)
        take_local(tv, utab, OUT_AT[8], me, count)
        for number, target in enumerate((qb, kb, vb)):
            qa[number * RANK : (number + 1) * RANK, :] = down_of(dtab, 2 + number)
            take_local(target, utab, OUT_AT[2 + number], me, count)
        take_local(oa, dtab, IN_AT[5], me, count)
        skip.wait(0)
        skip.forward()
        for name in ("q", "k", "v", "o"):
            shared[name].send_own(owns[name].at[half, :])

        @pl.when(core == 0)
        def _():
            words_w.send_own(ck_own)

        @pl.when(core == 1)
        def _():
            words_w.send_own(cv_own)

        skip.swap(0)

        skip.wait(1)
        skip.swap(1)
        cross_step(1)

        for number in (1, 2, 3):
            source = act_all.at[xor_place(dp, number)]
            push(source, source, msend.at[0, number - 1], mrecv.at[0, number - 1], dp_peers[number - 1]).wait_recv()
        for owner in range(4):
            @pl.when(dp == owner)
            def _(owner=owner):
                span_of = slice(owner * mod_rows, (owner + 1) * mod_rows)
                for sequence in range(4):
                    mod_slice[sequence : sequence + 1, :] = act_all[sequence, :, span_of]

        skip.wait(2)
        skip.swap(2)
        loads[3].wait()
        products = dot_nn(mod_slice[...].astype(BF), wm[...])
        for sequence in range(4):
            mod_out[sequence] = products[sequence : sequence + 1]
        backs = [
            push(mod_out.at[xor_place(dp, number)], mod_in.at[dp], msend.at[1, number - 1], mrecv.at[1, number - 1],
                 dp_peers[number - 1])
            for number in (1, 2, 3)
        ]
        for copy in backs:
            copy.start()
        mod_in[dp] = mod_out[dp]
        places[0].wait()
        skip.wait_swaps()
        cross_step(2)
        for load in loads[:3]:
            load.wait()

        def compute(number):
            @pl.when(number % each == 0)
            def _():
                here = rows_of(number // each, block)
                left = hid[here, :].astype(F32)
                right = lsk[here, :].astype(F32)
                mean = (jnp.sum(left, axis=-1, keepdims=True) + jnp.sum(right, axis=-1, keepdims=True)) / (2 * width)
                spread = jnp.sum((left - mean) ** 2, axis=-1, keepdims=True)
                spread += jnp.sum((right - mean) ** 2, axis=-1, keepdims=True)
                inverse = lax.rsqrt(spread / (2 * width) + NORM_EPS)
                for place in range(count):
                    @pl.when(me == place)
                    def _(place=place):
                        source = hid if place * span < width else lsk
                        start = place * span % width
                        part_x[...] = source[here, start : start + span].astype(F32)
                x = ((part_x[...] - mean) * inverse * pgain[...]).astype(BF)
                u = dot_nt(x, sa[...]).astype(BF)
                y = (dot_nt(x, wskip[...]) + dot_nn(u, up_of(utab, 0))).astype(BF)
                for piece in range(each):
                    partial_a[number + piece] = y[piece * chunk : (piece + 1) * chunk]

        def text_product():
            @pl.when(core == 0)
            def _():
                text_place(ck_own).wait()

            @pl.when(core == 1)
            def _():
                text_place(cv_own).wait()

            x = t_ref[...]
            y = dot_nt(x, wtext[...])

            @pl.when(core == 0)
            def _():
                z = y + dot_nn(dot_nt(x, down_of(dtab, 7)).astype(BF), tk[...])
                parts, sides = [], []
                for head in range(heads):
                    normal, inverse = stats(z[:, head * HD : (head + 1) * HD])
                    upper = inverse.astype(BF)
                    parts.append(normal.astype(BF))
                    sides += [upper, (inverse - upper.astype(F32)).astype(BF)]
                text_kv[0, me, :, :local] = jnp.concatenate(parts, axis=1)
                text_kv[0, me, :, local : local + 2 * heads] = jnp.concatenate(sides, axis=1)

            @pl.when(core == 1)
            def _():
                z = y + dot_nn(dot_nt(x, down_of(dtab, 8)).astype(BF), tv[...])
                text_kv[1, me, :, :local] = z.astype(BF)

        text_slots = text_kv.at[core]

        def finish(slot, total):
            here = rows_of(slot, chunk)
            skip_out[here, :] = total
            normal, _ = stats(total)
            attn_in[here, :] = (normal * gain[0:1, :] + shift_row[...]).astype(BF)

        def project(number, carry):
            here = rows_of(number, block)
            x = attn_in[here, :]
            u = dot_nt(x, qa[...]).astype(BF)
            yq = dot_nn(x, wq[...]) + dot_nn(u[:, :RANK], qb[...])
            yk = dot_nn(x, wk[...]) + dot_nn(u[:, RANK : 2 * RANK], kb[...])
            yv = (dot_nn(x, wv[...]) + dot_nn(u[:, 2 * RANK :], vb[...])).astype(BF)
            parts_q, parts_k = [], []
            for head in range(heads):
                span_of = slice(head * HD, (head + 1) * HD)
                normal, inverse = stats(yq[:, span_of])
                q_out[head, here, :] = normal.astype(BF)
                parts_q.append(inverse)
                normal, inverse = stats(yk[:, span_of])
                keys[core, head, here, :] = normal.astype(BF)
                parts_k.append(inverse)
                values[core, head, here, :] = yv[:, span_of]
            inv_q[here, :] = jnp.concatenate(parts_q, axis=1)
            inv_k[here, :] = jnp.concatenate(parts_k, axis=1)
            return carry

        def beside(number):
            @pl.when(number == 1 * pace)
            def _():
                for other in (1, 2, 3):
                    target = mod_in.at[xor_place(dp, other)]
                    push(target, target, msend.at[1, other - 1], mrecv.at[1, other - 1], dp_peers[other - 1]).wait_recv()
                mod_u = dot_nt(act_low, down_of(dtab, 1)).astype(BF)
                shift_row[...] = mod_in[0] + mod_in[1] + mod_in[2] + mod_in[3] + dot_nn(mod_u, up_of(utab, 1))

            @pl.when(number == 2 * pace)
            def _():
                for weight in (*shared.values(), words_w):
                    weight.wait(0)
                    weight.forward()
                for weight in (*shared.values(), words_w):
                    weight.wait(1)
                for weight in shared.values():
                    weight.swap(0)
                    weight.swap(1)

            @pl.when(number == 4 * pace)
            def _():
                cross_step(3)
                for weight in cross:
                    weight.send_own()

            @pl.when(number == 5 * pace)
            def _():
                for weight in (*shared.values(), words_w):
                    weight.wait(2)
                for weight in shared.values():
                    weight.swap(2)

            @pl.when(number == 7 * pace)
            def _():
                for weight in wide:
                    weight.send_own(up_own.at[half, :])
                for place in places[1:5]:
                    place.wait()
                for weight in shared.values():
                    weight.wait_swaps()
                project(0, 0)

            @pl.when(number == 8 * pace)
            def _():
                project(1, 0)

            @pl.when(number == steps + count - 3)
            def _():
                text_product()
                line_gather_step(text_line, 0, text_slots)

        line_reduce_all(reduce_line, steps, compute, partial_a, left_a, right_a, sr_a, sl_a, finish, beside)

        lax.fori_loop(2, tokens // block, project, 0)
        stores = [
            pltpu.make_async_copy(source, target, out_sem.at[number])
            for number, (source, target) in enumerate(
                ((skip_out, skip_hbm), (attn_in, attn_hbm), (wq, wq_hbm), (wk, wk_hbm), (wv, wv_hbm), (wo, wo_hbm))
            )
        ]
        for store in stores:
            store.start()

        swaps = [
            push(ref.at[core], ref.at[core], xsend.at[number], xrecv.at[number], peer)
            for number, ref in enumerate((keys, values))
        ]
        for swap in swaps:
            swap.start()
        line_gather_step(text_line, 1, text_slots)
        for weight in cross:
            weight.wait(0)
            weight.forward()
            weight.swap(0)
            weight.swap(3)
        for number, ref in enumerate((keys, values)):
            push(ref.at[1 - core], ref.at[1 - core], xsend.at[number], xrecv.at[number], peer).wait_recv()

        def attend(place, carry):
            dest = scatter_order(me, count, place)
            here = rows_of(dest, share)
            outs, logs = [], []
            for head in range(heads):
                q = q_out[head, here, :]
                s0 = dot_nt(q, keys[0, head]) * scale
                s1 = dot_nt(q, keys[1, head]) * scale
                top = jnp.maximum(jnp.max(s0, axis=-1, keepdims=True), jnp.max(s1, axis=-1, keepdims=True))
                e0 = jnp.exp(s0 - top)
                e1 = jnp.exp(s1 - top)
                total = jnp.sum(e0, axis=-1, keepdims=True) + jnp.sum(e1, axis=-1, keepdims=True)
                share_of = 1.0 / total
                p0 = (e0 * share_of).astype(BF)
                p1 = (e1 * share_of).astype(BF)
                outs.append(dot_nn(p0, values[0, head]) + dot_nn(p1, values[1, head]))
                logs.append(top + jnp.log(total))
            low = jnp.concatenate(outs, axis=1).astype(BF)
            low_out[here, :] = low
            log_out[here, :] = jnp.concatenate(logs, axis=1)
            u = dot_nt(low, oa[...]).astype(BF)
            partial_b[dest] = (dot_nt(low, wo[...]) + dot_nn(u, up_of(utab, 5))).astype(BF)

            @pl.when(place < count - 1)
            def _():
                line_scatter_step(scatter_line, place, partial_b, left_b, right_b, sr_b, sl_b)

            @pl.when(place == 0)
            def _():
                line_gather_step(text_line, 2, text_slots)

            @pl.when(place == 1)
            def _():
                for weight in cross:
                    weight.wait(1)
                    weight.swap(1)
                line_gather_step(text_line, 3, text_slots)
                push(text_slots, text_slots, tsend, trecv, peer).start()

            @pl.when(place == 2)
            def _():
                for weight in cross:
                    weight.wait(2)
                    weight.swap(2)

            return carry

        lax.fori_loop(0, count, attend, 0)
        line_scatter_finish(scatter_line, partial_b, left_b, right_b, sr_b, sl_b, summed)
        for weight in wide:
            weight.wait(0)
            weight.wait(1)
        others = text_kv.at[1 - core]
        push(others, others, tsend, trecv, peer).wait_recv()
        for weight in cross:
            weight.wait_swaps()
        places[5].wait()
        for store in stores:
            store.wait()
        for weight in (skip, *shared.values(), words_w, *cross):
            weight.drain()
        for weight in wide:
            weight.drain_own()
        for which, cross_line in enumerate(cross_lines):
            line_gather_drain(cross_line, cross_view(which))
        for copy in spread + backs:
            copy.wait_send()
        line_gather_drain(text_line, text_slots)
        push(text_slots, text_slots, tsend, trecv, peer).wait_send()
        for swap in swaps:
            swap.wait_send()

    names = ("skip", "q", "k", "v", "o", "ck", "cv", "cq", "co", "up")
    return call(
        kernel,
        [(weights[name], name in ("cq", "co", "up")) for name in names] + [(index, None)]
        + [(condition, True)] + [(array, False) for array in (hidden, long_skip, text, mod_weight)]
        + [(array, True) for array in (gain_halves, gain_rows, *tables)],
        [
            ((tokens, width), F32, False),
            ((tokens, width), BF, False),
            ((heads, tokens, HD), BF, True),
            ((2, heads, tokens, HD), BF, True),
            ((2, heads, tokens, HD), BF, True),
            ((tokens, local), BF, True),
            ((tokens, heads), F32, True),
            ((tokens, heads), F32, True),
            ((tokens, heads), F32, True),
            ((share, width), F32, True),
            ((4, 1, width + 128), F32, True),
            ((2, count, words, local + 32), BF, True),
        ]
        + [((width, local), BF, False) for _ in range(4)]
        + [((count, width, local), BF, False) for _ in range(2)]
        + [((width, units), BF, False)],
        [vmem(tokens, width), vmem(tokens, width), vmem(words, text_width), vmem(mod_rows, width), dma(4),
         vmem(tokens, width, dtype=F32), vmem(tokens, width)] + [vmem(width, local) for _ in range(4)]
        + [dma(6), vmem(1, width, dtype=F32), vmem(width, span), vmem(local, text_width), vmem(block, span, dtype=F32), vmem(1, span, dtype=F32),
         vmem(RANK, span), vmem(RANK, local), vmem(RANK, local), vmem(3 * RANK, width)]
        + [vmem(RANK, local) for _ in range(4)]
        + [vmem(4, 1, width, dtype=F32), vmem(4, mod_rows, dtype=F32),
         vmem(4, 1, width, dtype=F32)]
        + [vmem(steps, chunk, width) for _ in range(5)] + [vmem(count, share, width) for _ in range(5)]
        + [dma(10, 7), dma(10, 7), dma(10), dma(2, 3), dma(2, 3), dma(), dma(),
           dma(2), dma(2)]
        + [dma(steps) for _ in range(4)] + [dma(count) for _ in range(16)],
        collective=1,
        cost=cost_of(8 * tokens * width * local, 60e6),
    )


def attention_backward(count, heads, g_first, query, keys, values, low, logs, inv_q, inv_k, out_weight, tables):
    share, width = g_first.shape
    tokens = query.shape[1]
    local = low.shape[1]
    scale = HD ** (-0.5)

    def kernel(g_ref, *refs):
        sources, refs = refs[:10], refs[10:]
        (gq_low, gk_low, gv_low, gall, ga_o, gb_o, q_ref, k_ref, v_ref, low_ref, log_ref, iq_ref, ik_ref, wo, dtab, utab,
         gk_acc, gv_acc, swap_out, swap_in, ao, lsem, xsend, xrecv, *sems) = refs
        loads = [
            pltpu.make_async_copy(source, target, lsem.at[number])
            for number, (source, target) in enumerate(
                zip(sources, (q_ref, k_ref, v_ref, low_ref, log_ref, iq_ref, ik_ref, wo, dtab, utab))
            )
        ]
        for load in loads:
            load.start()
        me = lax.axis_index("tensor")
        core = lax.axis_index("ctx")
        peer = {"ctx": 1 - core}
        grad_line = Line(me, count, *sems)
        gall[me] = g_ref[...]
        greet(line_partners(me, count) + [(core >= 0, peer)])
        line_gather_step(grad_line, 0, gall)
        for ref in (ga_o, gb_o, gk_acc, gv_acc):
            ref[...] = jnp.zeros_like(ref)
        for load in loads:
            load.wait()
        take_local(ao, dtab, IN_AT[5], me, count)

        def attend(place):
            rows = rows_of(place, share)
            g = gall[place]
            go = dot_nt(g, up_of(utab, 5)).astype(BF)
            g_attn = (dot_nn(g, wo[...]) + dot_nn(go, ao[...])).astype(BF)
            low = low_ref[rows, :]
            uo = dot_nt(low, ao[...]).astype(BF)
            gb_o[...] += dot_tn(uo, g)
            ga_o[...] += dot_tn(go, low)
            parts = []
            for head in range(heads):
                gh = g_attn[:, head * HD : (head + 1) * HD]
                q = q_ref[head, rows, :]
                probs, grads = [], []
                inner = 0.0
                for half in range(2):
                    p = jnp.exp(dot_nt(q, k_ref[half, head]) * scale - log_ref[rows, head : head + 1])
                    dp = dot_nt(gh, v_ref[half, head])
                    inner = inner + jnp.sum(p * dp, axis=-1, keepdims=True)
                    probs.append(p)
                    grads.append(dp)
                dq = 0.0
                for half in range(2):
                    ds = (probs[half] * (grads[half] - inner)).astype(BF)
                    dq = dq + dot_nn(ds, k_ref[half, head])
                    gk_acc[half, head] += dot_tn(ds, q)
                    gv_acc[half, head] += dot_tn(probs[half].astype(BF), gh)
                parts.append(norm_backward(q.astype(F32), iq_ref[rows, head : head + 1], dq * scale))
            gq_low[rows, :] = jnp.concatenate(parts, axis=1).astype(BF)

        def gather(number, carry):
            @pl.when(number > 0)
            def _():
                line_gather_step(grad_line, number, gall)

            def side(which, inner):
                place = me + (2 * which - 1) * number

                @pl.when((place >= 0) & (place < count) & ((number > 0) | (which == 0)))
                def _():
                    attend(lax.clamp(0, place, count - 1))

                return inner

            return lax.fori_loop(0, 2, side, carry)

        lax.fori_loop(0, count, gather, 0)
        swaps = []
        for head in range(heads):
            swap_out[head, 0] = (gk_acc[1 - core, head] * scale).astype(BF)
            swap_out[head, 1] = gv_acc[1 - core, head].astype(BF)
            swaps.append(push(swap_out.at[head], swap_in.at[head], xsend.at[head], xrecv.at[head], peer))
            swaps[-1].start()
        line_gather_drain(grad_line, gall)
        for head in range(heads):
            at = slice(head * HD, (head + 1) * HD)
            swaps[head].wait_recv()
            dk = gk_acc[core, head] * scale + swap_in[head, 0].astype(F32)
            normal = k_ref[core, head].astype(F32)
            gk_low[:, at] = norm_backward(normal, ik_ref[:, head : head + 1], dk).astype(BF)
            gv_low[:, at] = (gv_acc[core, head] + swap_in[head, 1].astype(F32)).astype(BF)
        for swap in swaps:
            swap.wait_send()

    return call(
        kernel,
        [(g_first, True)]
        + [(array, False) for array in (query, keys, values, low, logs, inv_q, inv_k, out_weight, *tables)],
        [
            ((tokens, local), BF, True),
            ((tokens, local), BF, True),
            ((tokens, local), BF, True),
            ((count, share, width), BF, True),
            ((RANK, local), F32, True),
            ((RANK, width), F32, True),
        ],
        [pltpu.VMEM(array.shape, array.dtype)
         for array in (query, keys, values, low, logs, inv_q, inv_k, out_weight, *tables)]
        + [vmem(2, heads, tokens, HD, dtype=F32), vmem(2, heads, tokens, HD, dtype=F32), vmem(heads, 2, tokens, HD),
           vmem(heads, 2, tokens, HD), vmem(RANK, local), dma(10), dma(heads), dma(heads)]
        + [dma(count) for _ in range(4)],
        collective=4,
        cost=cost_of(16 * tokens * width * local, 60e6),
    )


EARLY_A, EARLY_B = IN_AT[2], OUT_AT[2]
EARLY = IN_AT[12] - EARLY_A + OUT_AT[12] - EARLY_B
LATE = EARLY_A + EARLY_B


def back_end(count, grads, projections, attn_in, g_first, skip_out, hidden, long_skip, weight, mod_weight, block_sum,
             gain_halves, gain_rows, tables, condition, act_all, wide_grads, local_down, local_up, stacked):
    tokens, width = hidden.shape
    local = grads[0].shape[1]
    span = weight.shape[-1]
    block = tokens // count
    chunk = min(CHUNK, block)
    pace = max(1, 64 // chunk)
    each = block // chunk
    steps = tokens // chunk
    own_rows = RANK // count
    half_e = -(-EARLY // 256) * 128
    half_l = -(-LATE // 256) * 128
    base = IN_AT[12] - EARLY_A
    mod_rows = mod_weight.shape[0]

    def early(column):
        return column - EARLY_A if column < IN_AT[12] else column - EARLY_A - EARLY_B

    wide_at, wide = [early(column) for column in wide_grads], list(wide_grads.values())
    local_at = [early(column) for column in local_down] + [early(IN_AT[12] + column) for column in local_up]
    own_grads = list(local_down.values()) + list(local_up.values())
    stacked_at, stack = [early(column) for column in stacked], list(stacked.values())

    def kernel(gq, gk, gv, wq, wk, wv, x_hbm, gf_hbm, skip_hbm, hid_hbm, lsk_hbm, hbm_w, wm_hbm, b_in, gains, gain, dtab,
               utab, cond, act_ref, *refs):
        wide_refs, refs = refs[: len(wide)], refs[len(wide) :]
        own_refs, refs = refs[: len(own_grads)], refs[len(own_grads) :]
        stack_refs, refs = refs[: len(stack)], refs[len(stack) :]
        (out_h, out_l, out_a, out_b, out_c, ball, w, x_ref, gf_ref, skip_ref, hid, lsk, wm, buf_h, buf_l, low, g_ref, qkv_a, bq, bk, bv, partial_g, left_g, right_g,
         sr_g, sl_g, table, late, swap_out, swap_in, partial_e, left_e, right_e, sr_e, sl_e, summed, late_out, late_in,
         partial_l, slots_l, slots, late_slots, other_out, other_in, later_out, later_in, shifts, shift_in, act_out, act_in, g_act, g_sum,
         wsem, osem, ssem, rsem, dsend, drecv, msend, mrecv, zsend, zrecv, *sems) = refs
        me = lax.axis_index("tensor")
        core = lax.axis_index("ctx")
        dp = lax.axis_index("dp")
        peer = {"ctx": 1 - core}
        grad_line = Line(me, count, *sems[:4])
        early_line = Line(me, count, *sems[4:8])
        block_line = Line(me, count, *sems[8:])
        peers = [{"dp": xor_place(dp, number)} for number in (1, 2, 3)]
        z_peers = [{"tensor": xor_place(me, number)} for number in range(1, count)]
        loads = [
            pltpu.make_async_copy(source, target, wsem.at[number])
            for number, (source, target) in enumerate(
                ((x_hbm, x_ref), (gf_hbm, gf_ref), (skip_hbm, skip_ref), (hid_hbm, hid), (lsk_hbm, lsk), (hbm_w, w),
                 (wm_hbm, wm))
            )
        ]
        for load in loads:
            load.start()
        ball[me] = b_in[...]
        everyone = [(core >= 0, device) for device in z_peers + peers + [peer]]
        greet_all(everyone)
        for number, target in enumerate((bq, bk, bv)):
            qkv_a[number * RANK : (number + 1) * RANK, :] = down_of(dtab, 2 + number)
            take_local(target, utab, OUT_AT[2 + number], me, count)
        g_sum[...] = jnp.zeros_like(g_sum)
        act_low = act_ref[dp, :, :width].astype(BF)

        def compute(number):
            @pl.when((number % each == 0) & (number > 0))
            def _():
                product(number)

        def product(number):
            rows = rows_of(number // each, block)
            gu = jnp.concatenate(
                [dot_nt(gq[rows, :], bq[...]), dot_nt(gk[rows, :], bk[...]), dot_nt(gv[rows, :], bv[...])], axis=1
            ).astype(BF)
            y = dot_nt(gq[rows, :], wq[...]) + dot_nt(gk[rows, :], wk[...]) + dot_nt(gv[rows, :], wv[...])
            y = (y + dot_nn(gu, qkv_a[...])).astype(BF)
            for piece in range(each):
                partial_g[number + piece] = y[piece * chunk : (piece + 1) * chunk]

        def finish(slot, total):
            g_ref[rows_of(slot, chunk), :] = total

        def skip_block(number):
            rows = rows_of(number, block)
            ga_in = g_ref[rows, :]
            g_sum[...] += jnp.sum(ga_in, axis=0, keepdims=True)
            normal, inverse = stats(skip_ref[rows, :])
            g_low = (
                gf_ref[number].astype(F32) + norm_backward(normal, inverse, ga_in * gain[0:1, :])
            ).astype(BF)
            left = hid[rows, :].astype(F32)
            right = lsk[rows, :].astype(F32)
            mean = (jnp.sum(left, axis=-1, keepdims=True) + jnp.sum(right, axis=-1, keepdims=True)) / (2 * width)
            left = left - mean
            right = right - mean
            spread = jnp.sum(left * left, axis=-1, keepdims=True) + jnp.sum(right * right, axis=-1, keepdims=True)
            inverse = lax.rsqrt(spread / (2 * width) + NORM_EPS)
            left = left * inverse
            right = right * inverse
            gu = dot_nt(g_low, up_of(utab, 0)).astype(BF)
            a_left, a_right = dtab[:, :width], dtab[:, width : 2 * width]

            @pl.when(number == me)
            def _():
                low_l = (left * gains[0:1, :]).astype(BF)
                low_r = (right * gains[1:2, :]).astype(BF)
                u = (dot_nt(low_l, a_left) + dot_nt(low_r, a_right)).astype(BF)
                late[:, :width] = dot_tn(gu, low_l)
                late[:, width : 2 * width] = dot_tn(gu, low_r)
                late[:, EARLY_A : EARLY_A + width] = dot_tn(u, g_low)

            for place in range(count):
                low[:, place * span : (place + 1) * span] = dot_nn(g_low, w[place])
            gl = (low[:, :width] + dot_nn(gu, a_left)) * gains[0:1, :]
            gr = (low[:, width:] + dot_nn(gu, a_right)) * gains[1:2, :]
            mean = (jnp.sum(gl, axis=-1, keepdims=True) + jnp.sum(gr, axis=-1, keepdims=True)) / (2 * width)
            inner = (
                jnp.sum(gl * left, axis=-1, keepdims=True) + jnp.sum(gr * right, axis=-1, keepdims=True)
            ) / (2 * width)
            buf_h[number] = inverse * (gl - mean - left * inner)
            buf_l[number] = inverse * (gr - mean - right * inner)
            pltpu.make_async_copy(buf_h.at[number], out_h.at[rows, :], osem.at[0, number]).start()
            pltpu.make_async_copy(buf_l.at[number], out_l.at[rows, :], osem.at[1, number]).start()

        swap = push(swap_out, swap_in, ssem.at[0], rsem.at[0], peer)
        sends = [
            push(slots.at[dp], slots.at[dp], dsend.at[0, number], drecv.at[0, number], device)
            for number, device in enumerate(peers)
        ]

        def early_step(number):
            line_scatter_step(early_line, number, partial_e, left_e, right_e, sr_e, sl_e)

        def beside(number):
            @pl.when(number == pace)
            def _():
                for load in loads:
                    load.wait()
                x = x_ref[...]
                u = dot_nt(x, qkv_a[...]).astype(BF)
                table[...] = jnp.zeros_like(table)
                late[...] = jnp.zeros_like(late)
                for start, ref in zip(wide_at, wide_refs):
                    table[:, start : start + ref.shape[1]] = ref[...]
                for start, ref in zip(stacked_at, stack_refs):
                    size = ref.shape[2]
                    for place in range(count):
                        table[:, start + place * size : start + (place + 1) * size] = ref[place]
                qkv_b = []
                for which, (grad, factor) in enumerate(((gq, bq), (gk, bk), (gv, bv))):
                    gu = dot_nt(grad[...], factor[...]).astype(BF)
                    table[:, which * width : (which + 1) * width] = dot_tn(gu, x)
                    qkv_b.append(dot_tn(u[:, which * RANK : (which + 1) * RANK], grad[...]))
                for place in range(count):
                    @pl.when(me == place)
                    def _(place=place):
                        for which, piece in enumerate(qkv_b):
                            start = base + which * width + place * local
                            table[:, start : start + local] = piece
                        for start, ref in zip(local_at, own_refs):
                            size = ref.shape[1]
                            table[:, start + place * size : start + (place + 1) * size] = ref[...]
                for which in range(2):
                    @pl.when(core == which)
                    def _(which=which):
                        swap_out[...] = table[:, (1 - which) * half_e : (2 - which) * half_e].astype(BF)

                swap.start()

            @pl.when(number == 3 * pace)
            def _():
                swap.wait()
                for which in range(2):
                    @pl.when(core == which)
                    def _(which=which):
                        for part in range(count):
                            at = slice(part * own_rows, (part + 1) * own_rows)
                            mine = table[at, which * half_e : (which + 1) * half_e]
                            partial_e[part] = (mine + swap_in[at, :].astype(F32)).astype(BF)

            @pl.when((number >= steps) & (number < steps + count - 1))
            def _():
                early_step(number - steps)

            @pl.when(number == steps - 1)
            def _():
                line_gather_step(block_line, 0, ball)

        def after(slot):
            @pl.when(slot % each == each - 1)
            def _():
                skip_block(slot // each)

        product(0)
        await_all(everyone)
        line_reduce_all(
            grad_line, steps, compute, partial_g, left_g, right_g, sr_g, sl_g, finish, beside, after
        )

        g_shift = g_sum[...]
        shift_in[0] = g_shift
        swap_shift = push(shift_in.at[0], shift_in.at[1], ssem.at[2], rsem.at[2], peer)
        swap_shift.start()
        mod_u = dot_nt(act_low, down_of(dtab, 1))
        once = jnp.where(me == 0, 1.0, 0.0)
        shift_u = dot_nt(g_shift.astype(BF), up_of(utab, 1))
        zeros_u, zeros_w = jnp.zeros((7, RANK), F32), jnp.zeros((7, width), F32)
        mod_a = jnp.concatenate([shift_u * once, zeros_u], axis=0).astype(BF)
        mod_b = jnp.concatenate([mod_u * once, zeros_u], axis=0).astype(BF)
        act_pad = jnp.concatenate([act_low.astype(F32), zeros_w], axis=0).astype(BF)
        shift_pad = jnp.concatenate([g_shift, zeros_w], axis=0).astype(BF)
        late[:, IN_AT[1] : IN_AT[2]] = dot_tn(mod_a, act_pad)
        late[:, EARLY_A + OUT_AT[1] : EARLY_A + OUT_AT[2]] = dot_tn(mod_b, shift_pad)
        for which in range(2):
            @pl.when(core == which)
            def _(which=which):
                late_out[...] = late[:, (1 - which) * half_l : (2 - which) * half_l].astype(BF)

        swap_late = push(late_out, late_in, ssem.at[1], rsem.at[1], peer)
        swap_late.start()
        line_gather_step(block_line, 1, ball)
        line_scatter_finish(early_line, partial_e, left_e, right_e, sr_e, sl_e, summed)
        slots[dp] = summed[...].astype(BF)
        for send in sends:
            send.start()
        swap_shift.wait()
        shifts[dp] = shift_in[0] + shift_in[1]
        shift_sends = [
            push(shifts.at[dp], shifts.at[dp], msend.at[0, number], mrecv.at[0, number], device)
            for number, device in enumerate(peers)
        ]
        for send in shift_sends:
            send.start()
        swap_late.wait()
        for which in range(2):
            @pl.when(core == which)
            def _(which=which):
                for part in range(count):
                    at = slice(part * own_rows, (part + 1) * own_rows)
                    mine = late[at, which * half_l : (which + 1) * half_l]
                    partial_l[part] = (mine + late_in[at, :].astype(F32)).astype(BF)

        late_sends = [
            push(partial_l.at[xor_place(me, number + 1)], slots_l.at[me], zsend.at[number], zrecv.at[number], device)
            for number, device in enumerate(z_peers)
        ]
        for send in late_sends:
            send.start()
        slots_l[me] = partial_l[me]
        line_gather_step(block_line, 2, ball)
        for number in (1, 2, 3):
            source = shifts.at[xor_place(dp, number)]
            push(source, source, msend.at[0, number - 1], mrecv.at[0, number - 1], peers[number - 1]).wait_recv()
        every = jnp.concatenate([shifts[sequence] for sequence in range(4)], axis=0).astype(BF)
        products = dot_nt(every, wm[...])
        for sequence in range(4):
            act_out[sequence] = products[sequence : sequence + 1]
        act_sends = [
            push(act_out.at[xor_place(dp, number)], act_in.at[dp], msend.at[1, number - 1], mrecv.at[1, number - 1],
                 peers[number - 1])
            for number in (1, 2, 3)
        ]
        for send in act_sends:
            send.start()
        for number in range(count - 1):
            arrived = slots_l.at[xor_place(me, number + 1)]
            push(arrived, arrived, zsend.at[number], zrecv.at[number], z_peers[number]).wait_recv()
        late_sum = slots_l[0].astype(F32)
        for place in range(1, count):
            late_sum = late_sum + slots_l[place].astype(F32)
        late_slots[dp] = late_sum.astype(BF)
        later_sends = [
            push(late_slots.at[dp], late_slots.at[dp], dsend.at[1, number], drecv.at[1, number], device)
            for number, device in enumerate(peers)
        ]
        for send in later_sends:
            send.start()

        def arrive(ref, which):
            for number in (1, 2, 3):
                source = ref.at[xor_place(dp, number)]
                push(source, source, dsend.at[which, number - 1], drecv.at[which, number - 1], peers[number - 1]).wait_recv()

        def total(ref, which):
            slot = (dp * 2 + which).astype(F32)
            result = jnp.zeros(ref.shape[1:], F32)
            for sequence in range(4):
                chosen = jnp.where(act_ref[sequence, :, width : width + 1] == slot, 1.0, 0.0)
                result = result + ref[sequence].astype(F32) * chosen
            return result

        arrive(slots, 0)
        other_out[...] = total(slots, 1 - core).astype(BF)
        last = push(other_out, other_in, ssem.at[3], rsem.at[3], peer)
        last.start()
        mine_e = total(slots, core)
        line_gather_step(block_line, 3, ball)
        arrive(late_slots, 1)
        later_out[...] = total(late_slots, 1 - core).astype(BF)
        latest = push(later_out, later_in, ssem.at[4], rsem.at[4], peer)
        latest.start()
        mine_l = total(late_slots, core)

        act_in[dp] = act_out[dp]
        for number in (1, 2, 3):
            source = act_in.at[xor_place(dp, number)]
            push(source, source, msend.at[1, number - 1], mrecv.at[1, number - 1], peers[number - 1]).wait_recv()
        for place in range(4):
            g_act[:, place * mod_rows : (place + 1) * mod_rows] = act_in[place]
        full_u = dot_nt(shifts[dp].astype(BF), up_of(utab, 1)).astype(BF)
        grad = g_act[...] + dot_nn(full_u, down_of(dtab, 1))
        value = cond[...].astype(F32)
        gate = 1.0 / (1.0 + jnp.exp(-value))
        out_c[...] = grad * gate * (1.0 + value * (1.0 - gate))

        def lay(mine, arrived, target):
            for which in range(2):
                @pl.when(core == which)
                def _(which=which):
                    target(which, mine)
                    target(1 - which, arrived[...].astype(F32))

        def lay_early(which, values):
            start = which * half_e
            low_a = max(0, min(base - start, half_e))
            if low_a:
                out_a[:, EARLY_A + start : EARLY_A + start + low_a] = values[:, :low_a]
            if low_a < half_e:
                at = EARLY_B + start + low_a - base
                out_b[:, at : at + min(half_e, EARLY - start) - low_a] = values[:, low_a : min(half_e, EARLY - start)]

        def lay_late(which, values):
            start = which * half_l
            low_a = max(0, min(EARLY_A - start, half_l))
            end = min(half_l, LATE - start)
            if low_a:
                out_a[:, start : start + low_a] = values[:, :low_a]
            if low_a < end:
                at = start + low_a - EARLY_A
                out_b[:, at : at + end - low_a] = values[:, low_a:end]

        last.wait_recv()
        lay(mine_e, other_in, lay_early)
        latest.wait_recv()
        lay(mine_l, later_in, lay_late)
        line_gather_drain(block_line, ball)
        last.wait_send()
        latest.wait_send()
        for send in sends + later_sends + shift_sends + act_sends + late_sends:
            send.wait_send()

        def drain(number, carry):
            rows = rows_of(number, block)
            pltpu.make_async_copy(buf_h.at[number], out_h.at[rows, :], osem.at[0, number]).wait()
            pltpu.make_async_copy(buf_l.at[number], out_l.at[rows, :], osem.at[1, number]).wait()
            return carry

        lax.fori_loop(0, count, drain, 0)

    part_e = (own_rows, half_e)
    part_l = (own_rows, half_l)
    return call(
        kernel,
        [(array, True) for array in (*grads, *projections)]
        + [(array, False) for array in (attn_in, g_first, skip_out, hidden, long_skip, weight, mod_weight)]
        + [(array, True) for array in (block_sum, gain_halves, gain_rows, *tables, condition, act_all, *wide, *own_grads,
                                       *stack)],
        [
            ((tokens, width), F32, False),
            ((tokens, width), F32, False),
            ((own_rows, IN_AT[12]), F32, True),
            ((own_rows, OUT_AT[12]), F32, True),
            ((1, width), F32, True),
            ((count, block, width), BF, True),
        ],
        [
            vmem(count, width, span),
            vmem(tokens, width), vmem(count, block, width), vmem(tokens, width, dtype=F32), vmem(tokens, width),
            vmem(tokens, width), vmem(mod_rows, width),
            vmem(count, block, width, dtype=F32),
            vmem(count, block, width, dtype=F32),
            vmem(block, 2 * width, dtype=F32),
            vmem(tokens, width, dtype=F32),
            vmem(3 * RANK, width),
            vmem(RANK, local), vmem(RANK, local), vmem(RANK, local),
        ]
        + [vmem(steps, chunk, width) for _ in range(5)]
        + [vmem(RANK, 2 * half_e, dtype=F32), vmem(RANK, 2 * half_l, dtype=F32), vmem(RANK, half_e), vmem(RANK, half_e)]
        + [vmem(count, *part_e) for _ in range(5)]
        + [vmem(*part_e, dtype=F32), vmem(RANK, half_l), vmem(RANK, half_l), vmem(count, *part_l), vmem(count, *part_l)]
        + [vmem(4, *part_e), vmem(4, *part_l), vmem(*part_e), vmem(*part_e), vmem(*part_l), vmem(*part_l)]
        + [vmem(4, 1, width, dtype=F32), vmem(2, 1, width, dtype=F32), vmem(4, 1, mod_rows, dtype=F32),
           vmem(4, 1, mod_rows, dtype=F32), vmem(1, width, dtype=F32), vmem(1, width, dtype=F32)]
        + [dma(7), dma(2, count), dma(5), dma(5), dma(2, 3), dma(2, 3), dma(2, 3), dma(2, 3), dma(count), dma(count)]
        + [dma(steps) for _ in range(4)] + [dma(count) for _ in range(8)],
        collective=5,
        cost=cost_of(4 * tokens * width * width, 30e6),
    )


def prepare(index, down_factor, up_factor, gain, transposed):
    def kernel(index_ref, down_ref, up_ref, gain_ref, *refs):
        count = len(transposed)
        weight_refs, (down_out, up_out, gain_out), outs = refs[:count], refs[count : count + 3], refs[count + 3 :]
        down_out[...] = down_ref[0]
        up_out[...] = up_ref[0]
        gain_out[0, :] = gain_ref[:MODEL_WIDTH]
        gain_out[1, :] = gain_ref[MODEL_WIDTH:]
        for source, target in zip(weight_refs, outs):
            target[...] = source[...].T

    def whole(shape):
        return pl.BlockSpec(shape, lambda step, index_ref: (0,) * len(shape))

    shapes = [down_factor.shape[1:], up_factor.shape[1:]]
    out_shapes = [(shape, BF) for shape in shapes] + [((2, MODEL_WIDTH), F32)]
    out_shapes += [(weight.shape[::-1], BF) for weight in transposed]
    return pl.pallas_call(
        kernel,
        grid_spec=pltpu.PrefetchScalarGridSpec(
            num_scalar_prefetch=1,
            grid=(1,),
            in_specs=[pl.BlockSpec((1, *shape), lambda step, index_ref: (index_ref[0], 0, 0)) for shape in shapes]
            + [whole((2 * MODEL_WIDTH,))] + [whole(weight.shape) for weight in transposed],
            out_specs=[whole(shape) for shape, _ in out_shapes],
        ),
        out_shape=[jax.ShapeDtypeStruct(shape, dtype) for shape, dtype in out_shapes],
        compiler_params=pltpu.CompilerParams(vmem_limit_bytes=VMEM_BYTES),
    )(index, down_factor, up_factor, gain, *transposed)


def fused_body(
    hidden,
    long_skip_input,
    condition,
    projected_text_tokens,
    sequence_adapter_index,
    skip_projection_weight,
    shift_modulation_weight,
    self_query_weight,
    self_key_weight,
    self_value_weight,
    attention_output_weight,
    cross_query_weight,
    cross_key_weight,
    cross_value_weight,
    cross_output_weight,
    feedforward_up_weight,
    feedforward_down_weight,
    skip_norm_gain,
    norm_gain_rows,
    adapter_down_factor,
    adapter_up_factor,
    cotangent,
):
    rank = lax.axis_index("tensor")
    count = lax.axis_size("tensor")
    core = lax.axis_index("ctx")
    dp = lax.axis_index("dp")
    hidden, long_skip, text, cot = hidden[0], long_skip_input[0], projected_text_tokens[0], cotangent[0]
    local = self_query_weight.shape[1]
    heads = local // HD
    down_table, up_table, gain_halves, skip_t, attn_out_t, cross_out_t = prepare(
        sequence_adapter_index, adapter_down_factor, adapter_up_factor, skip_norm_gain,
        (skip_projection_weight, attention_output_weight, cross_output_weight),
    )
    tables = (down_table, up_table)

    weights = {
        "skip": skip_t,
        "q": self_query_weight,
        "k": self_key_weight,
        "v": self_value_weight,
        "o": attn_out_t,
        "ck": cross_key_weight.T,
        "cv": cross_value_weight.T,
        "cq": cross_query_weight,
        "co": cross_out_t,
        "up": feedforward_up_weight,
        "dn": feedforward_down_weight.T,
    }
    (skip_out, attn_in, query, keys, values, low, logs, inv_q, inv_k, summed, act_all, text_kv, wq, wk, wv, wo, wcq, wco,
     wup) = front(
        count, heads, condition, sequence_adapter_index, hidden, long_skip, text, weights, shift_modulation_weight,
        gain_halves, norm_gain_rows, tables,
    )
    (g_first, block_sum, g_cq_a, g_cq_b, g_ck_a, g_ck_b, g_cv_a, g_cv_b, g_co_a, g_co_b, g_up_a, g_up_b, g_down_a, g_down_b,
     skip_all) = middle(
        count, heads, summed, skip_out, wcq, wco, wup, weights["dn"], weights["skip"], text_kv, text,
        cot.reshape(count, 2, -1, MODEL_WIDTH), norm_gain_rows, tables,
    )
    gq, gk, gv, g_first_all, g_o_a, g_o_b = attention_backward(
        count, heads, g_first, query, keys, values, low, logs, inv_q, inv_k, wo, tables
    )
    base = IN_AT[12]
    hidden_grad, skip_grad, grad_down, grad_up, g_condition, block_all = back_end(
        count, (gq, gk, gv), (wq, wk, wv), attn_in, g_first_all, skip_out, hidden, long_skip, skip_all,
        shift_modulation_weight, block_sum, gain_halves, norm_gain_rows, tables, condition, act_all,
        {
            IN_AT[6]: g_cq_a, IN_AT[7]: g_ck_a, IN_AT[8]: g_cv_a, IN_AT[10]: g_up_a,
            base + OUT_AT[5]: g_o_b, base + OUT_AT[9]: g_co_b, base + OUT_AT[11]: g_down_b,
        },
        {IN_AT[5]: g_o_a, IN_AT[11]: g_down_a},
        {OUT_AT[10]: g_up_b},
        {
            IN_AT[9]: g_co_a, base + OUT_AT[6]: g_cq_b, base + OUT_AT[7]: g_ck_b, base + OUT_AT[8]: g_cv_b,
        },
    )
    block_out = block_all.reshape(hidden.shape)
    size = MODEL_WIDTH // (2 * count)
    condition_gradient = lax.dynamic_slice_in_dim(g_condition[0], (core * count + rank) * size, size, 0)
    return (
        block_out[None],
        hidden_grad[None],
        skip_grad[None],
        condition_gradient,
        grad_down.reshape(-1),
        grad_up.reshape(-1),
    )


def solution(mesh):
    in_specs = (
        P("dp", "ctx", None),
        P("dp", "ctx", None),
        P("dp", None),
        P("dp", None, None),
        P("dp"),
        P("tensor", "dp"),
        P("dp", None),
        P("dp", "tensor"),
        P("dp", "tensor"),
        P("dp", "tensor"),
        P("tensor", "dp"),
        P("dp", "tensor"),
        P("dp", "tensor"),
        P("dp", "tensor"),
        P("tensor", "dp"),
        P("dp", "tensor"),
        P("tensor", "dp"),
        P(),
        P(),
        P(),
        P(),
        P("dp", "ctx", None),
    )
    out_specs = (
        P("dp", "ctx", None),
        P("dp", "ctx", None),
        P("dp", "ctx", None),
        P(("dp", "ctx", "tensor")),
        P(("dp", "ctx", "tensor")),
        P(("dp", "ctx", "tensor")),
    )
    shape = mesh.shape
    fused = shape["dp"] == 4 and shape["ctx"] == 2 and shape["tensor"] == 4
    return jax.shard_map(fused_body if fused else body, mesh=mesh, in_specs=in_specs, out_specs=out_specs, check_vma=False)
```

profile of v0, /device:TPU:0, one launch (start us, length us, event | category | flops | bytes accessed | tf_op | source)
XLA Modules:
  0.0 379.9 jit_solution(6803306223695063888)
XLA Ops:
  1.3 3.3 shard_map.253
  4.6 124.6 %shard_map.254 = (f32[512,1408]{1,0:T(8,128)}, bf16[512,1408]{1,0:T(8,128)(2,1)}, bf16[4,512,88]{2,1,0:T(8,128)(2,1)}, bf16[2,4,512,88]{3,2,1,0:T(8,128)(2,1)}, ...) custom-call(bf16[352,704]{1,0:T(8,128)(2,1)} %get-tuple-element.58.s, ...), custom_call_target="tpu_custom_call" | custom-call | flops 2030043136 | bytes 60000000 | tf_op jit(solution)/shard_map/pallas_call | solution.py:913
  129.2 110.2 %shard_map.255 = (bf16[128,1408]{1,0:T(8,128)(2,1)}, bf16[128,1408]{1,0:T(8,128)(2,1)}, f32[16,1408]{1,0:T(8,128)}, f32[4,16,352]{2,1,0:T(8,128)}, f32[16,1024]{...) custom-call(f32[128,1408]{1,0:T(8,128)} %get-tuple-element.64.sum_re, ...), custom_call_target="tpu_custom_call" | custom-call | flops 13287555072 | bytes 60000000 | tf_op jit(solution)/shard_map/pallas_call | solution.py:913
  239.4 37.6 %shard_map.256 = (bf16[512,352]{1,0:T(8,128)(2,1)}, bf16[512,352]{1,0:T(8,128)(2,1)}, bf16[512,352]{1,0:T(8,128)(2,1)}, bf16[4,128,1408]{2,1,0:T(8,128)(2,1)}, f32[16,352]{1,0:T(8,128)}, /*index=5*/f32[16,1408]{1,0:T(8,128)}) custom-call(bf16[128,1408]{1,0:T(8,128)(2,1)} %get-tuple-element.70.g_ref, bf16[4,512,88]{2,1,0:T(8,128)(2,1)} %get-tuple-element.71.refs_0_, ...), custom_call_target="tpu_custom_call" | custom-call | flops 4060086272 | bytes 60000000 | tf_op jit(solution)/shard_map/pallas_call | solution.py:913
  277.0 90.8 %shard_map.257 = (f32[512,1408]{1,0:T(8,128)}, f32[512,1408]{1,0:T(8,128)}, f32[4,22272]{1,0:T(4,128)}, f32[4,21632]{1,0:T(4,128)}, f32[1,1408]{1,0:T(1,128)}, /*index=5*/bf16[4,128,1408]{2,1,0:T(8,128)(2,1)}) custom-call(bf16[512,352]{1,0:T(8,128)(2,1)} %get-tuple-element.79.gq, bf16[512,352]{1,0:T(8,128)(2,1)} %get-tuple-element.80.gk, ...), custom_call_target="tpu_custom_call" | custom-call | flops 4060086272 | bytes 30000000 | tf_op jit(solution)/shard_map/pallas_call | solution.py:913
  367.8 0.0 copy-start.2
  367.8 2.0 reshape.19
  369.8 1.8 reshape.20
  371.6 1.3 constant_dynamic-slice_fusion
  372.9 0.0 copy-done.2
  372.9 0.0 copy-start.1
  372.9 1.1 copy.32
  374.0 1.2 copy-done.1
  375.3 0.0 copy-start
  375.3 1.6 copy.33
  376.8 1.3 copy-done
  378.1 1.6 copy.34
Async XLA Ops:
  367.8 5.1 %copy-start.2 = (bf16[4,128,1408]{2,1,0:T(8,128)(2,1)S(1)}, bf16[4,128,1408]{2,1,0:T(8,128)(2,1)}, u32[]{:S(2)}) copy-start(bf16[4,128,1408]{2,1,0:T(8,128)(2,1)} %get-tuple-element.104) | copy-start | bytes 4325380
  372.9 2.3 copy-start.1
  375.3 2.9 copy-start
where the time goes:
time: 384 us; the launch traced here: 380 us
  Pallas kernels  366 us (95%)
  local copies, waits for them, and re-layouts  11.9 us (3%)
    pallas_call x4, Pallas kernels, call(): pl.pallas_call(kernel, out_shape=[jax.ShapeDtypeStruct(shape, dtype) for...  363 us

commit v1 on v0

--- a/solution.py
+++ b/solution.py
@@ -2270,7 +2270,13 @@
         grad = g_act[...] + dot_nn(full_u, down_of(dtab, 1))
         value = cond[...].astype(F32)
         gate = 1.0 / (1.0 + jnp.exp(-value))
-        out_c[...] = grad * gate * (1.0 + value * (1.0 - gate))
+        whole_c = grad * gate * (1.0 + value * (1.0 - gate))
+        size_c = width // (2 * count)
+        for place in range(2 * count):
+            @pl.when(core * count + me == place)
+            def _(place=place):
+                out_c[...] = whole_c[:, place * size_c : (place + 1) * size_c]
+
 
         def lay(mine, arrived, target):
             for which in range(2):
@@ -2329,7 +2335,7 @@
             ((tokens, width), F32, False),
             ((own_rows, IN_AT[12]), F32, True),
             ((own_rows, OUT_AT[12]), F32, True),
-            ((1, width), F32, True),
+            ((1, width // (2 * count)), F32, True),
             ((count, block, width), BF, True),
         ],
         [
@@ -2466,8 +2472,7 @@
         },
     )
     block_out = block_all.reshape(hidden.shape)
-    size = MODEL_WIDTH // (2 * count)
-    condition_gradient = lax.dynamic_slice_in_dim(g_condition[0], (core * count + rank) * size, size, 0)
+    condition_gradient = g_condition[0]
     return (
         block_out[None],
         hidden_grad[None],

time: 384 us -> 384 us (level)
    unnamed x9 -> x10, local copies, waits for them, and re-layouts: 6.77 us -> 7.72 us
where the time goes in v1:
time: 384 us; the launch traced here: 379 us
  Pallas kernels  366 us (95%)
  local copies, waits for them, and re-layouts  11.4 us (3%)
    pallas_call x4, Pallas kernels, call(): pl.pallas_call(kernel, out_shape=[jax.ShapeDtypeStruct(shape, dtype) for...  363 us
    unnamed x10, local copies, waits for them, and re-layouts  7.72 us

profile of v1, /device:TPU:0, one launch (start us, length us, event | category | flops | bytes accessed | tf_op | source)
XLA Modules:
  0.0 379.4 jit_solution(11805537536614754636)
XLA Ops:
  1.3 3.3 shard_map.253
  4.6 124.6 %shard_map.254 = (f32[512,1408]{1,0:T(8,128)}, bf16[512,1408]{1,0:T(8,128)(2,1)}, bf16[4,512,88]{2,1,0:T(8,128)(2,1)}, bf16[2,4,512,88]{3,2,1,0:T(8,128)(2,1)}, ...) custom-call(bf16[352,704]{1,0:T(8,128)(2,1)} %get-tuple-element.58.s, ...), custom_call_target="tpu_custom_call" | custom-call | flops 2030043136 | bytes 60000000 | tf_op jit(solution)/shard_map/pallas_call | solution.py:913
  129.2 110.2 %shard_map.255 = (bf16[128,1408]{1,0:T(8,128)(2,1)}, bf16[128,1408]{1,0:T(8,128)(2,1)}, f32[16,1408]{1,0:T(8,128)}, f32[4,16,352]{2,1,0:T(8,128)}, f32[16,1024]{...) custom-call(f32[128,1408]{1,0:T(8,128)} %get-tuple-element.64.sum_re, ...), custom_call_target="tpu_custom_call" | custom-call | flops 13287555072 | bytes 60000000 | tf_op jit(solution)/shard_map/pallas_call | solution.py:913
  239.4 37.6 %shard_map.256 = (bf16[512,352]{1,0:T(8,128)(2,1)}, bf16[512,352]{1,0:T(8,128)(2,1)}, bf16[512,352]{1,0:T(8,128)(2,1)}, bf16[4,128,1408]{2,1,0:T(8,128)(2,1)}, f32[16,352]{1,0:T(8,128)}, /*index=5*/f32[16,1408]{1,0:T(8,128)}) custom-call(bf16[128,1408]{1,0:T(8,128)(2,1)} %get-tuple-element.70.g_ref, bf16[4,512,88]{2,1,0:T(8,128)(2,1)} %get-tuple-element.71.refs_0_, ...), custom_call_target="tpu_custom_call" | custom-call | flops 4060086272 | bytes 60000000 | tf_op jit(solution)/shard_map/pallas_call | solution.py:913
  277.0 90.8 %shard_map.257 = (f32[512,1408]{1,0:T(8,128)}, f32[512,1408]{1,0:T(8,128)}, f32[4,22272]{1,0:T(4,128)}, f32[4,21632]{1,0:T(4,128)}, f32[1,176]{1,0:T(1,128)}, /*index=5*/bf16[4,128,1408]{2,1,0:T(8,128)(2,1)}) custom-call(bf16[512,352]{1,0:T(8,128)(2,1)} %get-tuple-element.79.gq, bf16[512,352]{1,0:T(8,128)(2,1)} %get-tuple-element.80.gk, ...), custom_call_target="tpu_custom_call" | custom-call | flops 4060086272 | bytes 30000000 | tf_op jit(solution)/shard_map/pallas_call | solution.py:913
  367.8 1.8 reshape.19
  369.6 1.9 reshape.18
  371.5 0.0 copy-start.1
  371.5 2.7 copy.33
  374.2 0.0 copy-done.1
  374.2 0.0 copy-start
  374.2 1.6 copy.34
  375.8 1.3 copy-done
  377.1 0.0 copy-start.2
  377.1 1.6 copy.35
  378.7 0.0 copy-done.2
  378.7 0.6 copy.36
Async XLA Ops:
  371.5 2.7 copy-start.1
  374.2 2.9 copy-start
  377.1 1.6 copy-start.2
